TPU v7x, 32 devices: a whole 2x2x4 slice. The times are simulated.
32 devices in a mesh: dp: 8 (over y, x, core), seq: 4 (over z).
Axes of the slice: x: 2, y: 2, z: 4, core: 2. Of those that a mesh axis runs over, the one named last changes fastest.
Arguments:
- tokens: bfloat16 [8, 1024, 1024], P('dp', 'seq')
- cotangent: bfloat16 [8, 1024, 1024], P('dp', 'seq'), may hold values from -6 to 6
- valid_length: int32 [8], P('dp'), may hold values from 512 to 1024
- segment_ids: int32 [8, 1024], P('dp'), may hold values from 0 to 3, never falling along the last dimension, each value on 1 to 512 neighbouring positions
- piece_starts: int32 [8, 2], P('dp'), may hold values from 0 to 768, as said below
- norm1_gain: bfloat16 [1024], P(('dp', 'seq')), may hold values from 0.5 to 1.5
- norm1_bias: bfloat16 [1024], P(('dp', 'seq')), may hold values from -3 to 3
- qkv_weight: bfloat16 [1024, 3072], P(('dp', 'seq')), may hold values from -0.1875 to 0.1875
- qv_bias: bfloat16 [2048], P(('dp', 'seq')), may hold values from -3 to 3
- out_weight: bfloat16 [1024, 1024], P(('dp', 'seq')), may hold values from -1.5 to 1.5
- out_bias: bfloat16 [1024], P(('dp', 'seq')), may hold values from -3 to 3
- norm2_gain: bfloat16 [1024], P(('dp', 'seq')), may hold values from 0.5 to 1.5
- norm2_bias: bfloat16 [1024], P(('dp', 'seq')), may hold values from -3 to 3
- up_weight: bfloat16 [1024, 4096], P(('dp', 'seq')), may hold values from -0.1875 to 0.1875
- up_bias: bfloat16 [4096], P(('dp', 'seq')), may hold values from -3 to 3
- down_weight: bfloat16 [4096, 1024], P(('dp', 'seq')), may hold values from -0.09375 to 0.09375
- down_bias: bfloat16 [1024], P(('dp', 'seq')), may hold values from -3 to 3
Outputs:
- output: bfloat16 [8, 1024, 1024], P('dp', 'seq')
- tokens_grad: bfloat16 [8, 1024, 1024], P('dp', 'seq')
- grad_norm1_gain: float32 [1024], P(('dp', 'seq'))
- grad_norm1_bias: float32 [1024], P(('dp', 'seq'))
- grad_qkv_weight: float32 [1024, 3072], P(('dp', 'seq'))
- grad_qv_bias: float32 [2048], P(('dp', 'seq'))
- grad_out_weight: float32 [1024, 1024], P(('dp', 'seq'))
- grad_out_bias: float32 [1024], P(('dp', 'seq'))
- grad_norm2_gain: float32 [1024], P(('dp', 'seq'))
- grad_norm2_bias: float32 [1024], P(('dp', 'seq'))
- grad_up_weight: float32 [1024, 4096], P(('dp', 'seq'))
- grad_up_bias: float32 [4096], P(('dp', 'seq'))
- grad_down_weight: float32 [4096, 1024], P(('dp', 'seq'))
- grad_down_bias: float32 [1024], P(('dp', 'seq'))
- residual_rms: float32 [5], replicated
Inputs may be any that keep to these rules, and one draw needn't show every extreme that they name: `piece_starts`: piece p of a sequence starts at p * 512 plus an offset of 0 to 256, so pieces lie in order and never intersect.
All inputs are finite; a program needn't handle non-finite values.
Results may differ from a plain program's by a relative error of at most 0.012.
Values may be sent and summed in bfloat16 or wider, within the bound.
No kernel may reach another device: no remote copies, remote signals or barrier semaphores. Data moves between devices by JAX's collectives and lax.ppermute only.
A program may use at most 192 MiB of HBM per device.

v0:
```python
import jax
import jax.numpy as jnp
from jax import lax
from jax.sharding import PartitionSpec as P

HEAD_DIM = 64
PIECE = 256


gelu_scale = 0.7978845608028654
gelu_cubic = 0.044715


def layer_norm_parts(rows_in, gain, shift):
    mean_row = jnp.mean(rows_in, axis=-1, keepdims=True)
    centered = rows_in - mean_row
    inverse = lax.rsqrt(jnp.mean(centered * centered, axis=-1, keepdims=True) + 1e-05)
    unit_rows = centered * inverse
    return (unit_rows * gain + shift, unit_rows, inverse)


def layer_norm_back(grad_in, unit_rows, inverse, gain):
    scaled = grad_in * gain
    back_rows = inverse * (
        scaled
        - jnp.mean(scaled, axis=-1, keepdims=True)
        - unit_rows * jnp.mean(scaled * unit_rows, axis=-1, keepdims=True)
    )
    return (back_rows, jnp.sum(grad_in * unit_rows, axis=0), jnp.sum(grad_in, axis=0))


def gelu_parts(values):
    tangent = jnp.tanh(gelu_scale * (values + gelu_cubic * values * values * values))
    slope = 0.5 * (1.0 + tangent) + 0.5 * values * (1.0 - tangent * tangent) * gelu_scale * (
        1.0 + 3.0 * gelu_cubic * values * values
    )
    return (0.5 * values * (1.0 + tangent), slope)


def piece_labels(positions, starts):
    inside = (positions[:, :, None] >= starts[:, None, :]) & (
        positions[:, :, None] < starts[:, None, :] + PIECE
    )
    labels = jnp.arange(1, starts.shape[1] + 1, dtype=jnp.int32)
    return jnp.sum(jnp.where(inside, labels[None, None, :], 0), axis=2)


def visible(query_at, key_at, query_seg, key_seg, query_piece, key_piece, valid):
    query_pos = query_at[None, :, None]
    key_pos = key_at[None, None, :]
    limit_len = valid[:, None, None]
    same_seg = query_seg[:, :, None] == key_seg[:, None, :]
    together = (query_piece[:, :, None] == key_piece[:, None, :]) & (query_piece[:, :, None] > 0)
    rule_ok = same_seg & ((key_pos <= query_pos) | together)
    return (key_pos < limit_len) & ((query_pos >= limit_len) | rule_ok)


def split_heads(rows3):
    seq_count, length, model_width = rows3.shape
    return rows3.reshape(seq_count, length, model_width // HEAD_DIM, HEAD_DIM).transpose(2, 0, 1, 3)


def join_heads(stacked):
    head_count, seq_count, length, head_size = stacked.shape
    return stacked.transpose(1, 2, 0, 3).reshape(seq_count, length, head_count * head_size)


def per_device(
    tokens,
    cotangent,
    valid_length,
    segment_ids,
    piece_starts,
    norm1_gain,
    norm1_bias,
    qkv_weight,
    qv_bias,
    out_weight,
    out_bias,
    norm2_gain,
    norm2_bias,
    up_weight,
    up_bias,
    down_weight,
    down_bias,
):
    seq_count, local_len, model_width = tokens.shape
    full_len = segment_ids.shape[1]
    row_count = seq_count * local_len
    score_scale = HEAD_DIM ** (-0.5)
    offset = lax.axis_index("seq") * local_len
    query_at = offset + jnp.arange(local_len, dtype=jnp.int32)
    key_at = jnp.arange(full_len, dtype=jnp.int32)
    all_pieces = piece_labels(key_at[None, :], piece_starts)
    query_seg = lax.dynamic_slice_in_dim(segment_ids, offset, local_len, 1)
    query_piece = lax.dynamic_slice_in_dim(all_pieces, offset, local_len, 1)
    allowed = visible(
        query_at, key_at, query_seg, segment_ids, query_piece, all_pieces, valid_length
    )
    live_rows = (
        (query_at[None, :] < valid_length[:, None]).astype(jnp.float32).reshape(row_count, 1)
    )
    attn_full = (
        lax.all_gather(norm1_gain, ("dp", "seq"), axis=0, tiled=True),
        lax.all_gather(norm1_bias, ("dp", "seq"), axis=0, tiled=True),
        lax.all_gather(qkv_weight, ("dp", "seq"), axis=0, tiled=True),
        lax.all_gather(qv_bias, ("dp", "seq"), axis=0, tiled=True),
        lax.all_gather(out_weight, ("dp", "seq"), axis=0, tiled=True),
        lax.all_gather(out_bias, ("dp", "seq"), axis=0, tiled=True),
    )
    mlp_full = (
        lax.all_gather(norm2_gain, ("dp", "seq"), axis=0, tiled=True),
        lax.all_gather(norm2_bias, ("dp", "seq"), axis=0, tiled=True),
        lax.all_gather(up_weight, ("dp", "seq"), axis=0, tiled=True),
        lax.all_gather(up_bias, ("dp", "seq"), axis=0, tiled=True),
        lax.all_gather(down_weight, ("dp", "seq"), axis=0, tiled=True),
        lax.all_gather(down_bias, ("dp", "seq"), axis=0, tiled=True),
    )
    gain_one, shift_one, qkv_full, qv_full, out_full, out_shift = attn_full
    gain_two, shift_two, up_full, up_shift, down_full, down_shift = mlp_full
    tokens_f = tokens.reshape(row_count, model_width).astype(jnp.float32)
    normed_one, unit_one, inverse_one = layer_norm_parts(
        tokens_f, gain_one.astype(jnp.float32), shift_one.astype(jnp.float32)
    )
    normed_one = normed_one.astype(jnp.bfloat16)
    qkv_shift = jnp.concatenate(
        [qv_full[:model_width], jnp.zeros((model_width,), jnp.bfloat16), qv_full[model_width:]]
    ).astype(jnp.float32)
    qkv_rows = (
        jnp.dot(normed_one, qkv_full, preferred_element_type=jnp.float32) + qkv_shift
    ).astype(jnp.bfloat16)
    qkv_three = qkv_rows.reshape(seq_count, local_len, 3 * model_width)
    queries = qkv_three[:, :, :model_width]
    kv_all = lax.all_gather(qkv_three[:, :, model_width:], "seq", axis=1, tiled=True)
    query_heads = split_heads(queries)
    key_heads = split_heads(kv_all[:, :, :model_width])
    value_heads = split_heads(kv_all[:, :, model_width:])
    raw = (
        jnp.einsum("hsqd,hskd->hsqk", query_heads, key_heads, preferred_element_type=jnp.float32)
        * score_scale
    )
    row_top = jnp.max(jnp.where(allowed[None], raw, -1e30), axis=-1, keepdims=True)
    expo = jnp.exp(jnp.where(allowed[None], raw - row_top, -1e30))
    row_total = jnp.sum(expo, axis=-1, keepdims=True)
    attn_probs = (expo / row_total).astype(jnp.bfloat16)
    head_out = jnp.einsum(
        "hsqk,hskd->hsqd", attn_probs, value_heads, preferred_element_type=jnp.float32
    )
    head_outs = head_out.astype(jnp.bfloat16)
    lse_all = row_top[..., 0] + jnp.log(row_total[..., 0])
    attended = join_heads(head_outs).reshape(row_count, model_width)
    branch = jnp.dot(attended, out_full, preferred_element_type=jnp.float32) + out_shift.astype(
        jnp.float32
    )
    middle = tokens_f + branch
    normed_two, unit_two, inverse_two = layer_norm_parts(
        middle, gain_two.astype(jnp.float32), shift_two.astype(jnp.float32)
    )
    normed_two = normed_two.astype(jnp.bfloat16)
    hidden = jnp.dot(normed_two, up_full, preferred_element_type=jnp.float32) + up_shift.astype(
        jnp.float32
    )
    gelu_value, gelu_slope = gelu_parts(hidden)
    gated_act = gelu_value.astype(jnp.bfloat16)
    mlp_out = jnp.dot(gated_act, down_full, preferred_element_type=jnp.float32) + down_shift.astype(
        jnp.float32
    )
    result = middle + mlp_out
    output = result.astype(jnp.bfloat16).reshape(seq_count, local_len, model_width)
    squares = jnp.stack(
        [
            jnp.sum(live_rows * field * field)
            for field in (tokens_f, branch, middle, mlp_out, result)
        ]
    )
    square_sums, live_total = lax.psum((squares, jnp.sum(live_rows)), ("dp", "seq"))
    residual_rms = jnp.sqrt(square_sums / (live_total * model_width))
    gain_one_b, unused_one, qkv_back, unused_two, out_back, unused_three = attn_full
    gain_two_b, unused_four, up_back, unused_five, down_back, unused_six = mlp_full
    grad_out = cotangent.reshape(row_count, model_width) * live_rows.astype(jnp.bfloat16)
    grad_down_weight = jnp.einsum(
        "rf,rd->fd", gated_act, grad_out, preferred_element_type=jnp.float32
    )
    grad_down_bias = jnp.sum(grad_out.astype(jnp.float32), axis=0)
    grad_gated = jnp.einsum("rd,fd->rf", grad_out, down_back, preferred_element_type=jnp.float32)
    grad_hidden = (grad_gated * gelu_slope).astype(jnp.bfloat16)
    grad_up_weight = jnp.einsum(
        "rd,rf->df", normed_two, grad_hidden, preferred_element_type=jnp.float32
    )
    grad_up_bias = jnp.sum(grad_hidden.astype(jnp.float32), axis=0)
    grad_normed_two = jnp.einsum(
        "rf,df->rd", grad_hidden, up_back, preferred_element_type=jnp.float32
    )
    grad_mid_norm, grad_norm2_gain, grad_norm2_bias = layer_norm_back(
        grad_normed_two, unit_two, inverse_two, gain_two_b.astype(jnp.float32)
    )
    grad_middle = grad_out.astype(jnp.float32) + grad_mid_norm
    mlp_grads = (
        lax.psum_scatter(grad_norm2_gain, ("dp", "seq"), scatter_dimension=0, tiled=True),
        lax.psum_scatter(grad_norm2_bias, ("dp", "seq"), scatter_dimension=0, tiled=True),
        lax.psum_scatter(grad_up_weight, ("dp", "seq"), scatter_dimension=0, tiled=True),
        lax.psum_scatter(grad_up_bias, ("dp", "seq"), scatter_dimension=0, tiled=True),
        lax.psum_scatter(grad_down_weight, ("dp", "seq"), scatter_dimension=0, tiled=True),
        lax.psum_scatter(grad_down_bias, ("dp", "seq"), scatter_dimension=0, tiled=True),
    )
    grad_branch = grad_middle.astype(jnp.bfloat16)
    grad_out_weight = jnp.einsum(
        "rd,re->de", attended, grad_branch, preferred_element_type=jnp.float32
    )
    grad_out_bias = jnp.sum(grad_branch.astype(jnp.float32), axis=0)
    grad_attended = jnp.einsum(
        "re,de->rd", grad_branch, out_back, preferred_element_type=jnp.float32
    ).astype(jnp.bfloat16)
    grad_attended_three = grad_attended.reshape(seq_count, local_len, model_width)
    grad_heads = split_heads(grad_attended_three)
    raw = (
        jnp.einsum("hsqd,hskd->hsqk", query_heads, key_heads, preferred_element_type=jnp.float32)
        * score_scale
    )
    attn_probs = jnp.exp(jnp.where(allowed[None], raw - lse_all[..., None], -1e30))
    grad_probs = jnp.einsum(
        "hsqd,hskd->hsqk", grad_heads, value_heads, preferred_element_type=jnp.float32
    )
    attn_probs, grad_probs = (attn_probs, grad_probs)
    inner_sum = jnp.sum(attn_probs * grad_probs, axis=-1, keepdims=True)
    grad_scores = (attn_probs * (grad_probs - inner_sum)).astype(jnp.bfloat16)
    grad_query = (
        jnp.einsum("hsqk,hskd->hsqd", grad_scores, key_heads, preferred_element_type=jnp.float32)
        * score_scale
    )
    grad_key = (
        jnp.einsum("hsqk,hsqd->hskd", grad_scores, query_heads, preferred_element_type=jnp.float32)
        * score_scale
    )
    grad_value = jnp.einsum(
        "hsqk,hsqd->hskd",
        attn_probs.astype(jnp.bfloat16),
        grad_heads,
        preferred_element_type=jnp.float32,
    )
    partial_kv = jnp.concatenate([join_heads(grad_key), join_heads(grad_value)], axis=-1)
    local_kv = lax.psum_scatter(
        partial_kv.astype(jnp.bfloat16), "seq", scatter_dimension=1, tiled=True
    ).astype(jnp.float32)
    grad_qkv = jnp.concatenate(
        [
            join_heads(grad_query).reshape(row_count, model_width),
            local_kv.reshape(row_count, 2 * model_width),
        ],
        axis=-1,
    ).astype(jnp.bfloat16)
    grad_qkv_weight = jnp.einsum(
        "rd,re->de", normed_one, grad_qkv, preferred_element_type=jnp.float32
    )
    column_sums = jnp.sum(grad_qkv.astype(jnp.float32), axis=0)
    grad_qv_bias = jnp.concatenate([column_sums[:model_width], column_sums[2 * model_width :]])
    grad_normed_one = jnp.einsum(
        "re,de->rd", grad_qkv, qkv_back, preferred_element_type=jnp.float32
    )
    grad_in_norm, grad_norm1_gain, grad_norm1_bias = layer_norm_back(
        grad_normed_one, unit_one, inverse_one, gain_one_b.astype(jnp.float32)
    )
    tokens_grad = (
        (grad_middle + grad_in_norm).astype(jnp.bfloat16).reshape(seq_count, local_len, model_width)
    )
    attn_grads = (
        lax.psum_scatter(grad_norm1_gain, ("dp", "seq"), scatter_dimension=0, tiled=True),
        lax.psum_scatter(grad_norm1_bias, ("dp", "seq"), scatter_dimension=0, tiled=True),
        lax.psum_scatter(grad_qkv_weight, ("dp", "seq"), scatter_dimension=0, tiled=True),
        lax.psum_scatter(grad_qv_bias, ("dp", "seq"), scatter_dimension=0, tiled=True),
        lax.psum_scatter(grad_out_weight, ("dp", "seq"), scatter_dimension=0, tiled=True),
        lax.psum_scatter(grad_out_bias, ("dp", "seq"), scatter_dimension=0, tiled=True),
    )
    return (
        output,
        tokens_grad,
        attn_grads[0],
        attn_grads[1],
        attn_grads[2],
        attn_grads[3],
        attn_grads[4],
        attn_grads[5],
        mlp_grads[0],
        mlp_grads[1],
        mlp_grads[2],
        mlp_grads[3],
        mlp_grads[4],
        mlp_grads[5],
        residual_rms,
    )


def solution(mesh):
    return jax.shard_map(
        per_device,
        mesh=mesh,
        in_specs=(
            P("dp", "seq", None),
            P("dp", "seq", None),
            P("dp"),
            P("dp", None),
            P("dp", None),
            P(("dp", "seq")),
            P(("dp", "seq")),
            P(("dp", "seq"), None),
            P(("dp", "seq")),
            P(("dp", "seq"), None),
            P(("dp", "seq")),
            P(("dp", "seq")),
            P(("dp", "seq")),
            P(("dp", "seq"), None),
            P(("dp", "seq")),
            P(("dp", "seq"), None),
            P(("dp", "seq")),
        ),
        out_specs=(
            P("dp", "seq", None),
            P("dp", "seq", None),
            P(("dp", "seq")),
            P(("dp", "seq")),
            P(("dp", "seq"), None),
            P(("dp", "seq")),
            P(("dp", "seq"), None),
            P(("dp", "seq")),
            P(("dp", "seq")),
            P(("dp", "seq")),
            P(("dp", "seq"), None),
            P(("dp", "seq")),
            P(("dp", "seq"), None),
            P(("dp", "seq")),
            P(),
        ),
        check_vma=False,
    )
```

profile of v0, /device:TPU:0, one launch (start us, length us, event | category | flops | bytes accessed | tf_op | source)
XLA Modules:
  0.0 1575.6 jit_solution(2844633105114859951)
XLA Ops:
  13.8 42.5 %all-reduce.16 = (bf16[2048]{0:T(1024)(128)(2,1)S(1)}, bf16[1024]{0:T(1024)(128)(2,1)S(1)}, bf16[1024]{0:T(1024)(128)(2,1)S(1)}, bf16[1024]{0:T(1024)(128)(2,1)S...) all-reduce(bf16[2048]{0:T(1024)(128)(2,1)S(1)} %dynamic-update-slic, ...), channel_id=1, replica_groups=mesh['dp'=8,'seq'=4] {'dp','seq'}, use_global_device_ids=true, to_apply=%add.2 | all-reduce | flops 8192 | bytes 32768
  56.4 1.2 convert_reduce_fusion.3
  57.6 1.3 fusion.35
  58.9 24.0 %all-gather.7.cloned.1.call-done = bf16[1024,3072]{1,0:T(8,128)(2,1)} async-done(((bf16[32,3072]{1,0:T(8,128)(2,1)}), bf16[1024,3072]{1,0:T(8,128)(2,1)}) %all-gather.7.cloned.1.call-update) | async-done | bytes 6291472 | tf_op jit(solution)/shard_map/all_gather | solution.py:106
  82.9 4.9 fusion.13
  87.8 1.1 slice.35
  91.5 68.7 %all-gather = bf16[32,1,128]{2,1,0:T(2,128)(2,1)S(1)} all-gather(bf16[1,1,128]{2,1,0:T(2,128)(2,1)S(1)} %bitcast.163), channel_id=1, replica_groups=mesh['dp'=8,'seq'=4] {'dp','seq'}, dimensions={0}, use_global_device_ids=true | all-gather | bytes 8448 | tf_op jit(solution)/shard_map/all_gather | solution.py:115
  160.5 0.9 fusion.44
  161.7 6.7 all-gather.9.cloned.1.call-done
  168.5 4.0 fusion.69
  172.5 4.4 copy.45
  176.9 2.6 copy.46
  179.5 4.5 select_reduce_fusion
  183.9 4.9 fusion
  188.8 1.4 copy-done
  190.2 5.2 fusion.20
  195.4 30.9 %all-gather.11.cloned.1.call-done = bf16[1024,1024]{1,0:T(8,128)(2,1)} async-done(((bf16[32,1024]{1,0:T(8,128)(2,1)}), bf16[1024,1024]{1,0:T(8,128)(2,1)}) %all-gather.11.cloned.1.call-update) | async-done | bytes 2097168 | tf_op jit(solution)/shard_map/all_gather | solution.py:108
  226.3 3.3 fusion.67
  229.9 75.1 %all-gather.13.cloned.1.call-done = bf16[1024,4096]{1,0:T(8,128)(2,1)} async-done(((bf16[32,4096]{1,0:T(8,128)(2,1)}), bf16[1024,4096]{1,0:T(8,128)(2,1)}) %all-gather.13.cloned.1.call-update) | async-done | bytes 8388624 | tf_op jit(solution)/shard_map/all_gather | solution.py:114
  305.1 7.8 convolution_add_fusion
  312.9 70.7 %all-gather.15.cloned.1.call-done = bf16[4096,1024]{1,0:T(8,128)(2,1)} async-done(((bf16[128,1024]{1,0:T(8,128)(2,1)}), bf16[4096,1024]{1,0:T(8,128)(2,1)}) %all-gather.15.cloned.1.call-update) | async-done | bytes 8388624 | tf_op jit(solution)/shard_map/all_gather | solution.py:116
  383.6 11.3 convert_reduce_fusion
  394.9 6.5 fusion.72
  401.4 1.2 copy-done.17
  402.6 4.7 fusion.40
  407.9 1.6 convolution_convert_fusion
  409.5 2.0 copy.47
  411.5 10.3 fusion.14
  421.9 13.4 multiply_reduce_fusion
  435.2 12.0 multiply_convert_fusion
  447.2 1.6 multiply_convert_fusion.1
  448.8 1.6 copy-done.1
  450.5 2.5 pad_maximum_fusion
  453.0 1.0 copy-done.9
  454.0 2.7 fusion.55
  456.8 7.4 fusion.19
  464.2 64.4 %reduce-scatter.6.cloned.1.call-done = bf16[1,256,2048]{1,2,0:T(8,128)(2,1)} async-done(((bf16[1,1024,2048]{1,2,0:T(8,128)(2,1)}), bf16[1,256,2048]{1,2,0:T(8,128)(2,1)}) %reduce-scatter.6.cloned.1.call-update) | async-done | bytes 1048592 | tf_op jit(solution)/shard_map/reduce_scatter | solution.py:242
  528.6 7.8 fusion.46
  536.7 11.0 fusion.48
  547.7 9.8 fusion.66
  558.8 6.9 fusion.34
  565.7 3.3 stack.23
  569.6 42.7 %all-reduce.15 = (f32[1024]{0:T(1024)S(1)}, f32[1024]{0:T(1024)S(1)}, f32[2048]{0:T(1024)S(1)}, f32[1024]{0:T(1024)S(1)}, f32[1024]{0:T(1024)S(1)}, /*index=5*/f...) all-reduce(f32[1024]{0:T(1024)S(1)} %get-tuple-element.17, ...), channel_id=3, replica_groups=mesh['dp'=8,'seq'=4] {'dp','seq'}, use_global_device_ids=true, to_apply=%region_14.15.clone | all-reduce | flops 12294 | bytes 98352
  618.1 2.4 fusion.45
  620.6 60.6 %reduce-scatter.10.cloned.1.call-done = f32[32,1024]{1,0:T(8,128)} async-done(((f32[1024,1024]{1,0:T(8,128)}), f32[32,1024]{1,0:T(8,128)}) %reduce-scatter.10.cloned.1.call-update) | async-done | bytes 131088 | tf_op jit(solution)/shard_map/reduce_scatter | solution.py:271
  681.2 160.1 %reduce-scatter.8.cloned.1.call-done = f32[32,3072]{1,0:T(8,128)} async-done(((f32[1024,3072]{1,0:T(8,128)}), f32[32,3072]{1,0:T(8,128)}) %reduce-scatter.8.cloned.1.call-update) | async-done | bytes 393232 | tf_op jit(solution)/shard_map/reduce_scatter | solution.py:269
  841.2 362.4 %reduce-scatter.14.cloned.1.call-done = f32[128,1024]{1,0:T(8,128)} async-done(((f32[4096,1024]{1,0:T(8,128)}), f32[128,1024]{1,0:T(8,128)}) %reduce-scatter.14.cloned.1.call-update) | async-done | bytes 524304 | tf_op jit(solution)/shard_map/reduce_scatter | solution.py:203
  1203.7 364.7 %reduce-scatter.12.cloned.1.call-done = f32[32,4096]{1,0:T(8,128)} async-done(((f32[1024,4096]{1,0:T(8,128)}), f32[32,4096]{1,0:T(8,128)}) %reduce-scatter.12.cloned.1.call-update) | async-done | bytes 524304 | tf_op jit(solution)/shard_map/reduce_scatter | solution.py:201
  (111 shorter events, 17.3 us)
Async XLA Ops:
  7.2 75.7 %all-gather.7.cloned.1.call-start = ((), (), s32[]{:S(2)}) async-start(), calls=%async_computation.5 | async-start | bytes 6488064 | tf_op jit(solution)/shard_map/all_gather | solution.py:106
  7.9 160.6 %all-gather.9.cloned.1.call-start = ((), (), s32[]{:S(2)}) async-start(), calls=%async_computation.6 | async-start | bytes 5242880 | tf_op jit(solution)/shard_map/all_gather | solution.py:134
  58.9 32.6 %copy-start.15 = (bf16[128]{0:T(256)(128)(2,1)S(1)}, bf16[128]{0:T(256)(128)(2,1)}, u32[]{:S(2)}) copy-start(bf16[128]{0:T(256)(128)(2,1)} %param.31) | copy-start | bytes 772
  58.9 101.4 %copy-start.14 = (s32[1,1024]{1,0:T(1,128)S(1)}, s32[1,1024]{1,0:T(1,128)}, u32[]{:S(2)}) copy-start(s32[1,1024]{1,0:T(1,128)} %param.20) | copy-start | bytes 12292
  58.9 101.4 %copy-start.16 = (s32[1,2]{1,0:T(1,128)S(1)}, s32[1,2]{1,0:T(1,128)}, u32[]{:S(2)}) copy-start(s32[1,2]{1,0:T(1,128)} %param.21) | copy-start | bytes 28
  88.9 137.4 %all-gather.11.cloned.1.call-start = ((), (), s32[]{:S(2)}) async-start(), calls=%async_computation.7 | async-start | bytes 2162688 | tf_op jit(solution)/shard_map/all_gather | solution.py:108
  89.6 215.4 %all-gather.13.cloned.1.call-start = ((), (), s32[]{:S(2)}) async-start(), calls=%async_computation.8 | async-start | bytes 8650752 | tf_op jit(solution)/shard_map/all_gather | solution.py:114
  90.2 293.3 %all-gather.15.cloned.1.call-start = ((), (), s32[]{:S(2)}) async-start(), calls=%async_computation.9 | async-start | bytes 8650752 | tf_op jit(solution)/shard_map/all_gather | solution.py:116
  90.8 437.8 %reduce-scatter.6.cloned.1.call-start = ((), (), s32[]{:S(2)}) async-start(), calls=%async_computation.10 | async-start | bytes 5242880 | tf_op jit(solution)/shard_map/reduce_scatter | solution.py:242
  183.9 6.3 copy-start
  183.9 6.3 copy-start.4
  190.2 36.1 %copy-start.2 = (bf16[1,256,1024]{2,1,0:T(8,128)(2,1)S(1)}, bf16[1,256,1024]{2,1,0:T(8,128)(2,1)}, u32[]{:S(2)}) copy-start(bf16[1,256,1024]{2,1,0:T(8,128)(2,1)} %param.17) | copy-start | bytes 1572868
  195.4 117.5 %copy-start.8 = (bf16[16,256,64]{1,2,0:T(8,128)(2,1)}, bf16[16,256,64]{1,2,0:T(8,128)(2,1)S(1)}, u32[]{:S(2)}) copy-start(bf16[16,256,64]{1,2,0:T(8,128)(2,1)S(1)} %fusion.20) | copy-start | bytes 1572868
  305.1 78.5 %copy-start.12 = (bf16[1,256,1024]{2,1,0:T(8,128)(2,1)S(1)}, bf16[1,256,1024]{2,1,0:T(8,128)(2,1)}, u32[]{:S(2)}) copy-start(bf16[1,256,1024]{2,1,0:T(8,128)(2,1)} %param.18) | copy-start | bytes 1572868
  394.8 6.6 copy-start.10
  394.8 6.6 copy-start.6
  394.9 7.8 copy-start.17
  402.6 4.8 copy-start.13
  402.6 5.3 copy-start.3
  411.5 10.3 copy-start.5
  411.5 10.3 copy-start.11
  447.2 3.2 copy-start.1
  453.0 1.0 copy-start.9
  453.0 228.2 %reduce-scatter.10.cloned.1.call-start = ((), (), s32[]{:S(2)}) async-start(), calls=%async_computation.12 | async-start | bytes 4325376 | tf_op jit(solution)/shard_map/reduce_scatter | solution.py:271
  456.7 384.5 %reduce-scatter.8.cloned.1.call-start = ((), (), s32[]{:S(2)}) async-start(), calls=%async_computation.11 | async-start | bytes 12976128 | tf_op jit(solution)/shard_map/reduce_scatter | solution.py:269
  536.4 667.3 %reduce-scatter.14.cloned.1.call-start = ((), (), s32[]{:S(2)}) async-start(), calls=%async_computation.14 | async-start | bytes 17301504 | tf_op jit(solution)/shard_map/reduce_scatter | solution.py:203
  547.7 1020.7 %reduce-scatter.12.cloned.1.call-start = ((), (), s32[]{:S(2)}) async-start(), calls=%async_computation.13 | async-start | bytes 17301504 | tf_op jit(solution)/shard_map/reduce_scatter | solution.py:201
  557.6 1.2 copy-start.7
Sparse Core Ops, SparseCore 0:
  10.9 72.0 all-gather.6
  89.0 79.4 all-gather.8
  171.4 54.8 all-gather.10
  229.1 75.9 all-gather.12
  307.8 75.6 all-gather.14
  453.1 75.4 reduce-scatter.5
  531.4 149.7 reduce-scatter.9
  687.8 153.4 reduce-scatter.7
  844.1 359.5 reduce-scatter.13
  1206.4 361.9 reduce-scatter.11
where the time goes:
time: 1580 us
  waiting for transfers between devices  1220 us (77%)
  blocking collectives  154 us (10%)
  matrix products  121 us (8%)
  local copies, waits for them, and re-layouts  34.1 us (2%)
  other arithmetic  27.9 us (2%)
  between operations  16.4 us (1%)
    reduce_scatter x1, waiting for transfers between devices, per_device(): lax.psum_scatter(grad_up_weight, ('dp', 'seq'), scatter_dimension=0, tile...  365 us
    reduce_scatter x1, waiting for transfers between devices, per_device(): lax.psum_scatter(grad_down_weight, ('dp', 'seq'), scatter_dimension=0, ti...  362 us
    reduce_scatter x1, waiting for transfers between devices, per_device(): lax.psum_scatter(grad_qkv_weight, ('dp', 'seq'), scatter_dimension=0, til...  160 us
    unnamed x2, blocking collectives  85.2 us
    all_gather x1, waiting for transfers between devices, per_device(): lax.all_gather(up_weight, ('dp', 'seq'), axis=0, tiled=True)  75.1 us
    all_gather x1, waiting for transfers between devices, per_device(): lax.all_gather(down_weight, ('dp', 'seq'), axis=0, tiled=True)  70.7 us
    all_gather x1, blocking collectives, per_device(): lax.all_gather(up_bias, ('dp', 'seq'), axis=0, tiled=True)  68.7 us
    reduce_scatter x1, waiting for transfers between devices, per_device(): lax.psum_scatter(partial_kv.astype(jnp.bfloat16), 'seq', scatter_dimensio...  64.4 us
  transfers between devices with their start and end apart: 10, of which 10 were waited for; matrix products, arithmetic and copies ran while one was open for 7% of the time, Pallas kernels for 0%

commit v1 on v0

--- a/solution.py
+++ b/solution.py
@@ -63,6 +63,98 @@
 def join_heads(stacked):
     head_count, seq_count, length, head_size = stacked.shape
     return stacked.transpose(1, 2, 0, 3).reshape(seq_count, length, head_count * head_size)
+
+
+def swap(value, axis, bit, size):
+    return lax.ppermute(value, axis, [(i, i ^ bit) for i in range(size)])
+
+
+def far_bits(dp_size):
+    bits = [1 << i for i in range(1, dp_size.bit_length() - 1)]
+    half = (len(bits) + 1) // 2
+    return bits, bits[half:] + bits[:half]
+
+
+def place(pieces, me):
+    first = pieces[0]
+    out = jnp.zeros((len(pieces),) + first.shape, first.dtype)
+    for k, piece in pieces.items():
+        out = lax.dynamic_update_slice_in_dim(out, piece[None], jnp.bitwise_xor(me, k), 0)
+    return out
+
+
+def gather_rows(shard, dp_size, seq_size, dp_at, seq_at):
+    rows, cols = shard.shape
+    blocks = {0: shard}
+    for k in range(1, seq_size):
+        blocks[k] = swap(shard, "seq", k, seq_size)
+    local = place(blocks, seq_at).reshape(seq_size * rows, cols)
+    orders = far_bits(dp_size)
+    halves = []
+    for side, order in enumerate(orders):
+        part = local[:, side * (cols // 2) : (side + 1) * (cols // 2)]
+        pieces = {0: part}
+        for bit in order + [1]:
+            for k in list(pieces):
+                pieces[k ^ bit] = swap(pieces[k], "dp", bit, dp_size)
+        halves.append(place(pieces, dp_at).reshape(dp_size * seq_size * rows, cols // 2))
+    return jnp.concatenate(halves, axis=1)
+
+
+def split_bit(value, bit, axis_bits, me):
+    axis = axis_bits.index(bit)
+    mine = jnp.where(jnp.bitwise_and(me, bit) > 0, 1, 0)
+    keep = lax.dynamic_index_in_dim(value, mine, axis, keepdims=False)
+    send = lax.dynamic_index_in_dim(value, 1 - mine, axis, keepdims=False)
+    return keep, send, [b for b in axis_bits if b != bit]
+
+
+def scatter_rows(full, dp_size, seq_size, dp_at, seq_at, sent=jnp.bfloat16):
+    rows, cols = full.shape
+    own = rows // (dp_size * seq_size)
+    bits = [1 << i for i in reversed(range(dp_size.bit_length() - 1))]
+    value = full.reshape([2] * len(bits) + [seq_size * own, cols])
+    keep, send, left_bits = split_bit(value, 1, bits, dp_at)
+    value = keep + swap(send.astype(sent), "dp", 1, dp_size).astype(jnp.float32)
+    halves = []
+    for side, order in enumerate(far_bits(dp_size)):
+        part = value[..., side * (cols // 2) : (side + 1) * (cols // 2)]
+        part_bits = left_bits
+        for bit in order:
+            keep, send, part_bits = split_bit(part, bit, part_bits, dp_at)
+            part = keep + swap(send.astype(sent), "dp", bit, dp_size).astype(jnp.float32)
+        halves.append(part)
+    part = jnp.concatenate(halves, axis=1).reshape(seq_size, own, cols)
+    total = lax.dynamic_index_in_dim(part, seq_at, 0, keepdims=False)
+    part = part.astype(sent)
+    for k in range(1, seq_size):
+        send = lax.dynamic_index_in_dim(part, jnp.bitwise_xor(seq_at, k), 0, keepdims=False)
+        total = total + swap(send, "seq", k, seq_size).astype(jnp.float32)
+    return total
+
+
+def sum_all(value, dp_size, seq_size):
+    bit = 1
+    while bit < dp_size:
+        value = value + swap(value, "dp", bit, dp_size)
+        bit *= 2
+    bit = 1
+    while bit < seq_size:
+        value = value + swap(value, "seq", bit, seq_size)
+        bit *= 2
+    return value
+
+
+def pack_rows(vectors, devices):
+    return jnp.concatenate([v.reshape(devices, -1) for v in vectors], axis=1)
+
+
+def unpack_rows(packed, widths):
+    outs, at = [], 0
+    for width in widths:
+        outs.append(packed[:, at : at + width].reshape(-1))
+        at += width
+    return outs
 
 
 def per_device(
@@ -88,7 +180,9 @@
     full_len = segment_ids.shape[1]
     row_count = seq_count * local_len
     score_scale = HEAD_DIM ** (-0.5)
-    offset = lax.axis_index("seq") * local_len
+    dp_size, seq_size = lax.axis_size("dp"), lax.axis_size("seq")
+    dp_at, seq_at = lax.axis_index("dp"), lax.axis_index("seq")
+    offset = seq_at * local_len
     query_at = offset + jnp.arange(local_len, dtype=jnp.int32)
     key_at = jnp.arange(full_len, dtype=jnp.int32)
     all_pieces = piece_labels(key_at[None, :], piece_starts)
@@ -100,24 +194,18 @@
     live_rows = (
         (query_at[None, :] < valid_length[:, None]).astype(jnp.float32).reshape(row_count, 1)
     )
-    attn_full = (
-        lax.all_gather(norm1_gain, ("dp", "seq"), axis=0, tiled=True),
-        lax.all_gather(norm1_bias, ("dp", "seq"), axis=0, tiled=True),
-        lax.all_gather(qkv_weight, ("dp", "seq"), axis=0, tiled=True),
-        lax.all_gather(qv_bias, ("dp", "seq"), axis=0, tiled=True),
-        lax.all_gather(out_weight, ("dp", "seq"), axis=0, tiled=True),
-        lax.all_gather(out_bias, ("dp", "seq"), axis=0, tiled=True),
-    )
-    mlp_full = (
-        lax.all_gather(norm2_gain, ("dp", "seq"), axis=0, tiled=True),
-        lax.all_gather(norm2_bias, ("dp", "seq"), axis=0, tiled=True),
-        lax.all_gather(up_weight, ("dp", "seq"), axis=0, tiled=True),
-        lax.all_gather(up_bias, ("dp", "seq"), axis=0, tiled=True),
-        lax.all_gather(down_weight, ("dp", "seq"), axis=0, tiled=True),
-        lax.all_gather(down_bias, ("dp", "seq"), axis=0, tiled=True),
-    )
-    gain_one, shift_one, qkv_full, qv_full, out_full, out_shift = attn_full
-    gain_two, shift_two, up_full, up_shift, down_full, down_shift = mlp_full
+    vectors = (norm1_gain, norm1_bias, qv_bias, out_bias, norm2_gain, norm2_bias, up_bias, down_bias)
+    widths = [v.shape[0] for v in vectors]
+    gather = lambda shard: gather_rows(shard, dp_size, seq_size, dp_at, seq_at)
+    scatter = lambda full, **kw: scatter_rows(full, dp_size, seq_size, dp_at, seq_at, **kw)
+    packed = gather(pack_rows(vectors, 1))
+    gain_one, shift_one, qv_full, out_shift, gain_two, shift_two, up_shift, down_shift = unpack_rows(
+        packed, widths
+    )
+    qkv_full = gather(qkv_weight)
+    out_full = gather(out_weight)
+    up_full = gather(up_weight)
+    down_full = gather(down_weight)
     tokens_f = tokens.reshape(row_count, model_width).astype(jnp.float32)
     normed_one, unit_one, inverse_one = layer_norm_parts(
         tokens_f, gain_one.astype(jnp.float32), shift_one.astype(jnp.float32)
@@ -173,10 +261,12 @@
             for field in (tokens_f, branch, middle, mlp_out, result)
         ]
     )
-    square_sums, live_total = lax.psum((squares, jnp.sum(live_rows)), ("dp", "seq"))
+    counted = jnp.concatenate([squares, jnp.sum(live_rows)[None]])
+    counted = sum_all(jnp.pad(counted, (0, 122))[None], dp_size, seq_size)[0]
+    square_sums, live_total = counted[:5], counted[5]
     residual_rms = jnp.sqrt(square_sums / (live_total * model_width))
-    gain_one_b, unused_one, qkv_back, unused_two, out_back, unused_three = attn_full
-    gain_two_b, unused_four, up_back, unused_five, down_back, unused_six = mlp_full
+    qkv_back, out_back, up_back, down_back = qkv_full, out_full, up_full, down_full
+    gain_one_b, gain_two_b = gain_one, gain_two
     grad_out = cotangent.reshape(row_count, model_width) * live_rows.astype(jnp.bfloat16)
     grad_down_weight = jnp.einsum(
         "rf,rd->fd", gated_act, grad_out, preferred_element_type=jnp.float32
@@ -195,14 +285,8 @@
         grad_normed_two, unit_two, inverse_two, gain_two_b.astype(jnp.float32)
     )
     grad_middle = grad_out.astype(jnp.float32) + grad_mid_norm
-    mlp_grads = (
-        lax.psum_scatter(grad_norm2_gain, ("dp", "seq"), scatter_dimension=0, tiled=True),
-        lax.psum_scatter(grad_norm2_bias, ("dp", "seq"), scatter_dimension=0, tiled=True),
-        lax.psum_scatter(grad_up_weight, ("dp", "seq"), scatter_dimension=0, tiled=True),
-        lax.psum_scatter(grad_up_bias, ("dp", "seq"), scatter_dimension=0, tiled=True),
-        lax.psum_scatter(grad_down_weight, ("dp", "seq"), scatter_dimension=0, tiled=True),
-        lax.psum_scatter(grad_down_bias, ("dp", "seq"), scatter_dimension=0, tiled=True),
-    )
+    up_grad = scatter(grad_up_weight)
+    down_grad = scatter(grad_down_weight)
     grad_branch = grad_middle.astype(jnp.bfloat16)
     grad_out_weight = jnp.einsum(
         "rd,re->de", attended, grad_branch, preferred_element_type=jnp.float32
@@ -263,29 +347,37 @@
     tokens_grad = (
         (grad_middle + grad_in_norm).astype(jnp.bfloat16).reshape(seq_count, local_len, model_width)
     )
-    attn_grads = (
-        lax.psum_scatter(grad_norm1_gain, ("dp", "seq"), scatter_dimension=0, tiled=True),
-        lax.psum_scatter(grad_norm1_bias, ("dp", "seq"), scatter_dimension=0, tiled=True),
-        lax.psum_scatter(grad_qkv_weight, ("dp", "seq"), scatter_dimension=0, tiled=True),
-        lax.psum_scatter(grad_qv_bias, ("dp", "seq"), scatter_dimension=0, tiled=True),
-        lax.psum_scatter(grad_out_weight, ("dp", "seq"), scatter_dimension=0, tiled=True),
-        lax.psum_scatter(grad_out_bias, ("dp", "seq"), scatter_dimension=0, tiled=True),
+    qkv_grad = scatter(grad_qkv_weight)
+    out_grad = scatter(grad_out_weight)
+    vector_grads = (
+        grad_norm1_gain,
+        grad_norm1_bias,
+        grad_qv_bias,
+        grad_out_bias,
+        grad_norm2_gain,
+        grad_norm2_bias,
+        grad_up_bias,
+        grad_down_bias,
+    )
+    packed_grads = pack_rows(vector_grads, dp_size * seq_size)
+    n1g, n1b, qvb, ob, n2g, n2b, ub, db = unpack_rows(
+        scatter(packed_grads, sent=jnp.float32), widths
     )
     return (
         output,
         tokens_grad,
-        attn_grads[0],
-        attn_grads[1],
-        attn_grads[2],
-        attn_grads[3],
-        attn_grads[4],
-        attn_grads[5],
-        mlp_grads[0],
-        mlp_grads[1],
-        mlp_grads[2],
-        mlp_grads[3],
-        mlp_grads[4],
-        mlp_grads[5],
+        n1g,
+        n1b,
+        qkv_grad,
+        qvb,
+        out_grad,
+        ob,
+        n2g,
+        n2b,
+        up_grad,
+        ub,
+        down_grad,
+        db,
         residual_rms,
     )
 

time: 1580 us -> 736 us (0.47)
  waiting for transfers between devices: 1220 us -> 323 us
  blocking collectives: 154 us -> 0 us
  starting transfers between devices: 0.65 us -> 123 us
  local copies, waits for them, and re-layouts: 34.1 us -> 121 us
  matrix products: 121 us -> 81.5 us
  other arithmetic: 27.9 us -> 65.6 us
    reduce_scatter x4 -> x0, waiting for transfers between devices: 948 us -> none  [the longest x1 365 us: per_device(): lax.psum_scatter(grad_up_weight, ('dp', 'seq'), scatter_dimension=0, tile...]
    ppermute x0 -> x130, waiting for transfers between devices: none -> 300 us  [swap(): return lax.ppermute(value, axis, [(i, i ^ bit) for i in range(size)])]
    all_gather x4 -> x0, waiting for transfers between devices: 201 us -> none  [the longest x1 75.1 us: per_device(): lax.all_gather(up_weight, ('dp', 'seq'), axis=0, tiled=True)]
    ppermute x0 -> x130, starting transfers between devices: none -> 123 us  [swap(): return lax.ppermute(value, axis, [(i, i ^ bit) for i in range(size)])]
    unnamed x2 -> x0, blocking collectives: 85.2 us -> none
    all_gather x1 -> x0, blocking collectives: 68.7 us -> none  [per_device(): lax.all_gather(up_bias, ('dp', 'seq'), axis=0, tiled=True)]
    reduce_scatter x1, waiting for transfers between devices: 64.4 us -> 0.01 us  [per_device(): lax.psum_scatter(partial_kv.astype(jnp.bfloat16), 'seq', scatter_dimensio...]
    dynamic_update_slice x0 -> x99, local copies, waits for them, and re-layouts: none -> 40.6 us  [place(): lax.dynamic_update_slice_in_dim(out, piece[None], jnp.bitwise_xor(me, k), 0)]
  transfers between devices with their start and end apart: 10 -> 132, of which waited for: 10 -> 68; matrix products, arithmetic and copies ran while one was open for 7% -> 21% of each run, Pallas kernels for 0% -> 0%
where the time goes in v1:
time: 736 us; the launch traced here: 732 us
  waiting for transfers between devices  323 us (44%)
  starting transfers between devices  123 us (17%)
  local copies, waits for them, and re-layouts  121 us (16%)
  matrix products  81.5 us (11%)
  other arithmetic  65.6 us (9%)
  between operations  17.7 us (2%)
    ppermute x130, waiting for transfers between devices, swap(): return lax.ppermute(value, axis, [(i, i ^ bit) for i in range(size)])  300 us
    ppermute x130, starting transfers between devices, swap(): return lax.ppermute(value, axis, [(i, i ^ bit) for i in range(size)])  123 us
    dynamic_update_slice x99, local copies, waits for them, and re-layouts, place(): lax.dynamic_update_slice_in_dim(out, piece[None], jnp.bitwise_xor(me, k), 0)  40.6 us
    all_gather x1, waiting for transfers between devices, per_device(): lax.all_gather(qkv_three[:, :, model_width:], 'seq', axis=1, tiled=True)  22.7 us
    add x5, other arithmetic, scatter_rows(): value = keep + swap(send.astype(sent), 'dp', 1, dp_size).astype(jnp.float32)  18.8 us
    unnamed x136, local copies, waits for them, and re-layouts  16 us
  transfers between devices with their start and end apart: 132, of which 68 were waited for; matrix products, arithmetic and copies ran while one was open for 21% of the time, Pallas kernels for 0%

profile of v1, /device:TPU:0, one launch (start us, length us, event | category | flops | bytes accessed | tf_op | source)
XLA Modules:
  0.0 731.6 jit_solution(891595509398985930)
XLA Ops:
  69.2 4.1 collective-permute-done.29
  74.1 4.3 collective-permute-done.37
  80.0 4.8 collective-permute-done.38
  90.3 4.4 collective-permute-done.31
  104.5 16.5 %collective-permute-done.52 = bf16[32,4096]{1,0:T(8,128)(2,1)S(1)} collective-permute-done((bf16[32,4096]{1,0:T(8,128)(2,1)S(1)}, bf16[32,4096]{1,0:T(8,128)(2,1)S(1)}, u32[]{:S(2)}, u32[]{:S(2)}) %collective-permute-start.52) | collective-permute-done | bytes 262176 | tf_op jit(solution)/shard_map/ppermute | solution.py:69
  125.2 7.0 collective-permute-done.69
  148.7 4.5 collective-permute-done.21
  153.2 5.6 collective-permute-done.13
  161.0 8.5 %collective-permute-done.61 = bf16[128,2048]{1,0:T(8,128)(2,1)} collective-permute-done((bf16[128,2048]{1,0:T(8,128)(2,1)S(1)}, bf16[128,2048]{1,0:T(8,128)(2,1)}, u32[]{:S(2)}, u32[]{:S(2)}) %collective-permute-start.61) | collective-permute-done | bytes 524320 | tf_op jit(solution)/shard_map/ppermute | solution.py:69
  173.8 6.1 collective-permute-done.78
  180.2 4.3 collective-permute-done.79
  186.1 9.7 %collective-permute-done.71 = bf16[512,512]{1,0:T(8,128)(2,1)S(1)} collective-permute-done((bf16[512,512]{1,0:T(8,128)(2,1)}, bf16[512,512]{1,0:T(8,128)(2,1)S(1)}, u32[]{:S(2)}, u32[]{:S(2)}) %collective-permute-start.71) | collective-permute-done | bytes 524320 | tf_op jit(solution)/shard_map/ppermute | solution.py:69
  196.0 8.6 %collective-permute-done.54 = bf16[128,2048]{1,0:T(8,128)(2,1)S(1)} collective-permute-done((bf16[128,2048]{1,0:T(8,128)(2,1)}, bf16[128,2048]{1,0:T(8,128)(2,1)S(1)}, u32[]{:S(2)}, u32[]{:S(2)}) %collective-permute-start.54) | collective-permute-done | bytes 524320 | tf_op jit(solution)/shard_map/ppermute | solution.py:69
  204.7 5.8 collective-permute-done.55
  212.0 9.1 %collective-permute-done.22 = bf16[128,1536]{1,0:T(8,128)(2,1)S(1)} collective-permute-done((bf16[128,1536]{1,0:T(8,128)(2,1)S(1)}, bf16[128,1536]{1,0:T(8,128)(2,1)S(1)}, u32[]{:S(2)}, u32[]{:S(2)}) %collective-permute-start.22) | collective-permute-done | bytes 393248 | tf_op jit(solution)/shard_map/ppermute | solution.py:69
  226.1 10.6 %collective-permute-done.15 = bf16[128,1536]{1,0:T(8,128)(2,1)S(1)} collective-permute-done((bf16[128,1536]{1,0:T(8,128)(2,1)S(1)}, bf16[128,1536]{1,0:T(8,128)(2,1)S(1)}, u32[]{:S(2)}, u32[]{:S(2)}) %collective-permute-start.15) | collective-permute-done | bytes 393248 | tf_op jit(solution)/shard_map/ppermute | solution.py:69
  240.1 12.6 %collective-permute-done.63 = bf16[128,2048]{1,0:T(8,128)(2,1)} collective-permute-done((bf16[128,2048]{1,0:T(8,128)(2,1)}, bf16[128,2048]{1,0:T(8,128)(2,1)}, u32[]{:S(2)}, u32[]{:S(2)}) %collective-permute-start.63) | collective-permute-done | bytes 524320 | tf_op jit(solution)/shard_map/ppermute | solution.py:69
  265.5 10.0 %collective-permute-done.56 = bf16[128,2048]{1,0:T(8,128)(2,1)} collective-permute-done((bf16[128,2048]{1,0:T(8,128)(2,1)}, bf16[128,2048]{1,0:T(8,128)(2,1)}, u32[]{:S(2)}, u32[]{:S(2)}) %collective-permute-start.56) | collective-permute-done | bytes 524320 | tf_op jit(solution)/shard_map/ppermute | solution.py:69
  283.1 9.0 %collective-permute-done.80 = bf16[512,512]{1,0:T(8,128)(2,1)} collective-permute-done((bf16[512,512]{1,0:T(8,128)(2,1)}, bf16[512,512]{1,0:T(8,128)(2,1)}, u32[]{:S(2)}, u32[]{:S(2)}) %collective-permute-start.80) | collective-permute-done | bytes 524320 | tf_op jit(solution)/shard_map/ppermute | solution.py:69
  298.6 7.0 collective-permute-done.73
  319.7 22.7 %all-gather.2.cloned.1.call-done = bf16[1,1024,2048]{2,1,0:T(8,128)(2,1)} async-done(((bf16[1,256,2048]{2,1,0:T(8,128)(2,1)}), bf16[1,1024,2048]{2,1,0:T(8,128)(2,1)}) %all-gather.2.cloned.1.call-update) | async-done | bytes 4194320 | tf_op jit(solution)/shard_map/all_gather | solution.py:222
  342.4 4.0 fusion.155
  346.3 4.0 copy.60
  353.0 4.5 select_reduce_fusion
  357.4 4.9 fusion
  363.7 5.2 fusion.44
  371.7 7.7 %fusion.20 = (bf16[4096,256]{0,1:T(8,128)(2,1)}, f32[256,4096]{1,0:T(8,128)}) fusion(f32[4096]{0:T(1024)S(1)} %copy-done.61, bf16[1024,2048]{1,0:T(8,128)(2,1)} %bitcast.625, bf16[1024,2048]{1,0:T(8,128)(2,1)S(1)} %bitcast.623, f32[256,1024]{1,0:T(8,128)S(1)} %get-tuple-element.34, f32[1024]{0:T(1024)S(1)} %reshape.891, f32[1024]{0:T(1024)S(1)} %reshape.890, ...), kind=kOutput, calls=%fused_computation.38 | convolution fusion | flops 2176057344 | bytes 15755264 | tf_op jit(solution)/shard_map/dot_general | solution.py:248
  379.5 6.2 convert_reduce_fusion
  388.6 7.1 fusion.64
  398.4 10.1 %fusion.33 = bf16[16,1024,64]{1,2,0:T(8,128)(2,1)} fusion(bf16[16,256,64]{1,2,0:T(8,128)(2,1)S(1)} %bitcast.640, f32[16,256,1024]{2,1,0:T(8,128)} %copy-done, f32[16,256]{1,0:T(8,128)S(1)} %log_add_fusion, pred[256,1024]{1,0:T(8,128)(4,1)S(1)} %fusion.73), kind=kOutput, calls=%fused_computation.70 | convolution fusion | flops 554696704 | bytes 19677184 | tf_op jit(solution)/shard_map/hsqk,hsqd->hskd/dot_general | solution.py:319
  408.5 13.7 %multiply_reduce_fusion = (f32[16,256]{1,0:T(8,128)S(1)}, f32[16,256,1024]{2,1,0:T(8,128)}) fusion(f32[16,256,1024]{2,1,0:T(8,128)} %copy-done, f32[16,256]{1,0:T(8,128)S(1)} %log_add_fusion, pred[256,1024]{1,0:T(8,128)(4,1)S(1)} %fusion.73, bf16[16,256,64]{1,2,0:T(8,128)(2,1)S(1)} %bitcast.641, bf16[16,1024,64]{1,2,0:T(8,128)(2,1)S(1)} %bitcast.610), kind=kOutput, calls=%fused_computation.1 | convolution fusion | flops 557838336 | bytes 36470784 | tf_op jit(solution)/shard_map/hsqd,hskd->hsqk/dot_general | solution.py:305
  448.6 12.2 %multiply_convert_fusion = bf16[16,256,1024]{2,1,0:T(8,128)(2,1)S(1)} fusion(f32[16,256,1024]{2,1,0:T(8,128)} %get-tuple-element.97, f32[16,256,1024]{2,1,0:T(8,128)} %copy-done, f32[16,256]{1,0:T(8,128)S(1)} %get-tuple-element.96, f32[16,256]{1,0:T(8,128)S(1)} %log_add_fusion, pred[256,1024]{1,0:T(8,128)(4,1)S(1)} %fusion.73), kind=kLoop, calls=%fused_computation | loop fusion | flops 25165824 | bytes 42237952 | tf_op jit(solution)/shard_map/convert_element_type | solution.py:310
  465.9 4.0 copy.63
  497.1 6.1 bitcast_add_fusion
  508.7 5.8 bitcast_add_fusion.1
  520.9 11.0 %collective-permute-done.120 = bf16[2,512,512]{2,1,0:T(8,128)(2,1)} collective-permute-done((bf16[2,512,512]{2,1,0:T(8,128)(2,1)}, bf16[2,512,512]{2,1,0:T(8,128)(2,1)}, u32[]{:S(2)}, u32[]{:S(2)}) %collective-permute-start.120) | collective-permute-done | bytes 1048608 | tf_op jit(solution)/shard_map/ppermute | solution.py:69
  540.2 10.8 %collective-permute-done.112 = bf16[2,128,2048]{2,1,0:T(8,128)(2,1)S(1)} collective-permute-done((bf16[2,128,2048]{2,1,0:T(8,128)(2,1)S(1)}, bf16[2,128,2048]{2,1,0:T(8,128)(2,1)S(1)}, u32[]{:S(2)}, u32[]{:S(2)}) %collective-permute-start.112) | collective-permute-done | bytes 1048608 | tf_op jit(solution)/shard_map/ppermute | solution.py:69
  557.3 6.4 collective-permute-done.121
  567.6 7.9 %collective-permute-done.113 = bf16[128,2048]{1,0:T(8,128)(2,1)S(1)} collective-permute-done((bf16[128,2048]{1,0:T(8,128)(2,1)S(1)}, bf16[128,2048]{1,0:T(8,128)(2,1)S(1)}, u32[]{:S(2)}, u32[]{:S(2)}) %collective-permute-start.113) | collective-permute-done | bytes 524320 | tf_op jit(solution)/shard_map/ppermute | solution.py:69
  588.3 14.8 %collective-permute-start.114 = (bf16[32,4096]{1,0:T(8,128)(2,1)S(1)}, bf16[32,4096]{1,0:T(8,128)(2,1)S(1)}, u32[]{:S(2)}, u32[]{:S(2)}) collective-permute-start(bf16[32,4096]{1,0:T(8,128)(2,1)S(1)} %get-tuple-element.51), channel_id=1, source_target_pairs={{0,1},{1,0},{2,3},{3,2},{4,5},{5,4},{6,7},{7,6},{8,9},{9,8},{10,11... | collective-permute-start | bytes 786440 | tf_op jit(solution)/shard_map/ppermute | solution.py:69
  604.7 7.6 %collective-permute-done.123 = bf16[128,1024]{1,0:T(8,128)(2,1)S(1)} collective-permute-done((bf16[128,1024]{1,0:T(8,128)(2,1)S(1)}, bf16[128,1024]{1,0:T(8,128)(2,1)S(1)}, u32[]{:S(2)}, u32[]{:S(2)}) %collective-permute-start.123) | collective-permute-done | bytes 262176 | tf_op jit(solution)/shard_map/ppermute | solution.py:69
  613.3 10.2 %collective-permute-done.115 = bf16[32,4096]{1,0:T(8,128)(2,1)S(1)} collective-permute-done((bf16[32,4096]{1,0:T(8,128)(2,1)S(1)}, bf16[32,4096]{1,0:T(8,128)(2,1)S(1)}, u32[]{:S(2)}, u32[]{:S(2)}) %collective-permute-start.115) | collective-permute-done | bytes 262176 | tf_op jit(solution)/shard_map/ppermute | solution.py:69
  624.5 5.1 fusion.23
  637.3 4.6 copy-done.3
  679.4 4.6 bitcast_add_fusion.2
  688.0 12.0 %collective-permute-done.96 = bf16[2,128,1536]{2,1,0:T(8,128)(2,1)S(1)} collective-permute-done((bf16[2,128,1536]{2,1,0:T(8,128)(2,1)S(1)}, bf16[2,128,1536]{2,1,0:T(8,128)(2,1)S(1)}, u32[]{:S(2)}, u32[]{:S(2)}) %collective-permute-start.96) | collective-permute-done | bytes 786464 | tf_op jit(solution)/shard_map/ppermute | solution.py:69
  704.0 4.4 collective-permute-done.97
  719.2 4.4 collective-permute-done.99
  (645 shorter events, 339.6 us)
Async XLA Ops:
  7.2 335.1 %all-gather.2.cloned.1.call-start = ((), (), s32[]{:S(2)}) async-start(), calls=%async_computation.1 | async-start | bytes 5242880 | tf_op jit(solution)/shard_map/all_gather | solution.py:222
  8.2 22.0 %collective-permute-start = (bf16[1,384]{1,0:T(2,128)(2,1)S(1)}, bf16[1,384]{1,0:T(2,128)(2,1)S(1)}, u32[]{:S(2)}, u32[]{:S(2)}) collective-permute-start(bf16[1,384]{1,0:T(2,128)(2,1)S(1)} %concatenate.92), channel_id=1, source_target_pairs={{0,1},{1,0},{2,3},{3,2},{4,5},{5,4},{6,7},{7,6},{8,9},{9,8},{10,11... | collective-permute-start | bytes 2312 | tf_op jit(solution)/shard_map/ppermute | solution.py:69
  11.3 18.9 %collective-permute-start.1 = (bf16[1,384]{1,0:T(2,128)(2,1)S(1)}, bf16[1,384]{1,0:T(2,128)(2,1)S(1)}, u32[]{:S(2)}, u32[]{:S(2)}) collective-permute-start(bf16[1,384]{1,0:T(2,128)(2,1)S(1)} %concatenate.92), channel_id=1, source_target_pairs={{0,2},{1,3},{2,0},{3,1},{4,6},{5,7},{6,4},{7,5},{8,10},{9,11},{10,... | collective-permute-start | bytes 2312 | tf_op jit(solution)/shard_map/ppermute | solution.py:69
  13.9 16.3 %collective-permute-start.2 = (bf16[1,384]{1,0:T(2,128)(2,1)S(1)}, bf16[1,384]{1,0:T(2,128)(2,1)S(1)}, u32[]{:S(2)}, u32[]{:S(2)}) collective-permute-start(bf16[1,384]{1,0:T(2,128)(2,1)S(1)} %concatenate.92), channel_id=1, source_target_pairs={{0,3},{1,2},{2,1},{3,0},{4,7},{5,6},{6,5},{7,4},{8,11},{9,10},{10,... | collective-permute-start | bytes 2312 | tf_op jit(solution)/shard_map/ppermute | solution.py:69
  13.9 80.9 %collective-permute-start.10 = (bf16[32,3072]{1,0:T(8,128)(2,1)}, bf16[32,3072]{1,0:T(8,128)(2,1)}, u32[]{:S(2)}, u32[]{:S(2)}) collective-permute-start(bf16[32,3072]{1,0:T(8,128)(2,1)} %param.24), channel_id=1, source_target_pairs={{0,1},{1,0},{2,3},{3,2},{4,5},{5,4},{6,7},{7,6},{8,9},{9,8},{10,11... | collective-permute-start | bytes 589832 | tf_op jit(solution)/shard_map/ppermute | solution.py:69
  14.8 82.5 %collective-permute-start.11 = (bf16[32,3072]{1,0:T(8,128)(2,1)}, bf16[32,3072]{1,0:T(8,128)(2,1)}, u32[]{:S(2)}, u32[]{:S(2)}) collective-permute-start(bf16[32,3072]{1,0:T(8,128)(2,1)} %param.24), channel_id=1, source_target_pairs={{0,2},{1,3},{2,0},{3,1},{4,6},{5,7},{6,4},{7,5},{8,10},{9,11},{10,... | collective-permute-start | bytes 589832 | tf_op jit(solution)/shard_map/ppermute | solution.py:69
  30.1 70.2 %collective-permute-start.12 = (bf16[32,3072]{1,0:T(8,128)(2,1)}, bf16[32,3072]{1,0:T(8,128)(2,1)}, u32[]{:S(2)}, u32[]{:S(2)}) collective-permute-start(bf16[32,3072]{1,0:T(8,128)(2,1)} %param.24), channel_id=1, source_target_pairs={{0,3},{1,2},{2,1},{3,0},{4,7},{5,6},{6,5},{7,4},{8,11},{9,10},{10,... | collective-permute-start | bytes 589832 | tf_op jit(solution)/shard_map/ppermute | solution.py:69
  34.4 16.1 %collective-permute-start.47 = (bf16[4,192]{1,0:T(4,128)(2,1)S(1)}, bf16[4,192]{1,0:T(4,128)(2,1)S(1)}, u32[]{:S(2)}, u32[]{:S(2)}) collective-permute-start(bf16[4,192]{1,0:T(4,128)(2,1)S(1)} %get-tuple-element.85), channel_id=1, source_target_pairs={{0,4},{4,0},{8,12},{12,8},{16,20},{20,16},{24,28},{28,24},{1,5},{5... | collective-permute-start | bytes 4616 | tf_op jit(solution)/shard_map/ppermute | solution.py:69
  67.7 35.2 %collective-permute-start.51 = (bf16[32,4096]{1,0:T(8,128)(2,1)}, bf16[32,4096]{1,0:T(8,128)(2,1)S(1)}, u32[]{:S(2)}, u32[]{:S(2)}) collective-permute-start(bf16[32,4096]{1,0:T(8,128)(2,1)} %param.30), channel_id=1, source_target_pairs={{0,1},{1,0},{2,3},{3,2},{4,5},{5,4},{6,7},{7,6},{8,9},{9,8},{10,11... | collective-permute-start | bytes 786440 | tf_op jit(solution)/shard_map/ppermute | solution.py:69
  94.7 26.2 %collective-permute-start.52 = (bf16[32,4096]{1,0:T(8,128)(2,1)S(1)}, bf16[32,4096]{1,0:T(8,128)(2,1)S(1)}, u32[]{:S(2)}, u32[]{:S(2)}) collective-permute-start(bf16[32,4096]{1,0:T(8,128)(2,1)S(1)} %copy-done.50), channel_id=1, source_target_pairs={{0,2},{1,3},{2,0},{3,1},{4,6},{5,7},{6,4},{7,5},{8,10},{9,11},{10,... | collective-permute-start | bytes 786440 | tf_op jit(solution)/shard_map/ppermute | solution.py:69
  94.8 26.2 %collective-permute-start.53 = (bf16[32,4096]{1,0:T(8,128)(2,1)S(1)}, bf16[32,4096]{1,0:T(8,128)(2,1)S(1)}, u32[]{:S(2)}, u32[]{:S(2)}) collective-permute-start(bf16[32,4096]{1,0:T(8,128)(2,1)S(1)} %copy-done.50), channel_id=1, source_target_pairs={{0,3},{1,2},{2,1},{3,0},{4,7},{5,6},{6,5},{7,4},{8,11},{9,10},{10,... | collective-permute-start | bytes 786440 | tf_op jit(solution)/shard_map/ppermute | solution.py:69
  97.3 26.4 %collective-permute-start.68 = (bf16[128,1024]{1,0:T(8,128)(2,1)S(1)}, bf16[128,1024]{1,0:T(8,128)(2,1)S(1)}, u32[]{:S(2)}, u32[]{:S(2)}) collective-permute-start(bf16[128,1024]{1,0:T(8,128)(2,1)S(1)} %copy-done.52), channel_id=1, source_target_pairs={{0,1},{1,0},{2,3},{3,2},{4,5},{5,4},{6,7},{7,6},{8,9},{9,8},{10,11... | collective-permute-start | bytes 786440 | tf_op jit(solution)/shard_map/ppermute | solution.py:69
  100.3 31.9 %collective-permute-start.69 = (bf16[128,1024]{1,0:T(8,128)(2,1)S(1)}, bf16[128,1024]{1,0:T(8,128)(2,1)S(1)}, u32[]{:S(2)}, u32[]{:S(2)}) collective-permute-start(bf16[128,1024]{1,0:T(8,128)(2,1)S(1)} %copy-done.52), channel_id=1, source_target_pairs={{0,2},{1,3},{2,0},{3,1},{4,6},{5,7},{6,4},{7,5},{8,10},{9,11},{10,... | collective-permute-start | bytes 786440 | tf_op jit(solution)/shard_map/ppermute | solution.py:69
  102.9 29.3 %collective-permute-start.70 = (bf16[128,1024]{1,0:T(8,128)(2,1)S(1)}, bf16[128,1024]{1,0:T(8,128)(2,1)S(1)}, u32[]{:S(2)}, u32[]{:S(2)}) collective-permute-start(bf16[128,1024]{1,0:T(8,128)(2,1)S(1)} %copy-done.52), channel_id=1, source_target_pairs={{0,3},{1,2},{2,1},{3,0},{4,7},{5,6},{6,5},{7,4},{8,11},{9,10},{10,... | collective-permute-start | bytes 786440 | tf_op jit(solution)/shard_map/ppermute | solution.py:69
  121.0 21.7 %collective-permute-start.33 = (bf16[128,512]{1,0:T(8,128)(2,1)S(1)}, bf16[128,512]{1,0:T(8,128)(2,1)S(1)}, u32[]{:S(2)}, u32[]{:S(2)}) collective-permute-start(bf16[128,512]{1,0:T(8,128)(2,1)S(1)} %get-tuple-element.68), channel_id=1, source_target_pairs={{0,4},{4,0},{8,12},{12,8},{16,20},{20,16},{24,28},{28,24},{1,5},{5... | collective-permute-start | bytes 393224 | tf_op jit(solution)/shard_map/ppermute | solution.py:69
  142.7 78.5 %collective-permute-start.23 = (bf16[128,1536]{1,0:T(8,128)(2,1)S(1)}, bf16[128,1536]{1,0:T(8,128)(2,1)S(1)}, u32[]{:S(2)}, u32[]{:S(2)}) collective-permute-start(bf16[128,1536]{1,0:T(8,128)(2,1)S(1)} %get-tuple-element.62), channel_id=1, source_target_pairs={{0,4},{4,0},{8,12},{12,8},{16,20},{20,16},{24,28},{28,24},{1,5},{5... | collective-permute-start | bytes 1179656 | tf_op jit(solution)/shard_map/ppermute | solution.py:69
  142.8 16.1 %collective-permute-start.13 = (bf16[128,1536]{1,0:T(8,128)(2,1)S(1)}, bf16[128,1536]{1,0:T(8,128)(2,1)S(1)}, u32[]{:S(2)}, u32[]{:S(2)}) collective-permute-start(bf16[128,1536]{1,0:T(8,128)(2,1)S(1)} %get-tuple-element.61), channel_id=1, source_target_pairs={{0,8},{4,12},{8,0},{12,4},{16,24},{20,28},{24,16},{28,20},{1,9},{5... | collective-permute-start | bytes 1179656 | tf_op jit(solution)/shard_map/ppermute | solution.py:69
  148.6 88.1 %collective-permute-start.16 = (bf16[128,1536]{1,0:T(8,128)(2,1)S(1)}, bf16[128,1536]{1,0:T(8,128)(2,1)S(1)}, u32[]{:S(2)}, u32[]{:S(2)}) collective-permute-start(bf16[128,1536]{1,0:T(8,128)(2,1)S(1)} %get-tuple-element.61), channel_id=1, source_target_pairs={{0,4},{4,0},{8,12},{12,8},{16,20},{20,16},{24,28},{28,24},{1,5},{5... | collective-permute-start | bytes 1179656 | tf_op jit(solution)/shard_map/ppermute | solution.py:69
  153.1 16.4 %collective-permute-start.61 = (bf16[128,2048]{1,0:T(8,128)(2,1)S(1)}, bf16[128,2048]{1,0:T(8,128)(2,1)}, u32[]{:S(2)}, u32[]{:S(2)}) collective-permute-start(bf16[128,2048]{1,0:T(8,128)(2,1)S(1)} %get-tuple-element.55), channel_id=1, source_target_pairs={{0,16},{4,20},{8,24},{12,28},{16,0},{20,4},{24,8},{28,12},{1,17},{... | collective-permute-start | bytes 1572872 | tf_op jit(solution)/shard_map/ppermute | solution.py:69
  160.4 19.5 %collective-permute-start.78 = (bf16[512,512]{1,0:T(8,128)(2,1)}, bf16[512,512]{1,0:T(8,128)(2,1)S(1)}, u32[]{:S(2)}, u32[]{:S(2)}) collective-permute-start(bf16[512,512]{1,0:T(8,128)(2,1)} %get-tuple-element.57), channel_id=1, source_target_pairs={{0,16},{4,20},{8,24},{12,28},{16,0},{20,4},{24,8},{28,12},{1,17},{... | collective-permute-start | bytes 1572872 | tf_op jit(solution)/shard_map/ppermute | solution.py:69
  172.1 23.7 %collective-permute-start.71 = (bf16[512,512]{1,0:T(8,128)(2,1)}, bf16[512,512]{1,0:T(8,128)(2,1)S(1)}, u32[]{:S(2)}, u32[]{:S(2)}) collective-permute-start(bf16[512,512]{1,0:T(8,128)(2,1)} %get-tuple-element.56), channel_id=1, source_target_pairs={{0,8},{4,12},{8,0},{12,4},{16,24},{20,28},{24,16},{28,20},{1,9},{5... | collective-permute-start | bytes 1572872 | tf_op jit(solution)/shard_map/ppermute | solution.py:69
  179.9 15.9 %collective-permute-start.72 = (bf16[512,512]{1,0:T(8,128)(2,1)}, bf16[512,512]{1,0:T(8,128)(2,1)S(1)}, u32[]{:S(2)}, u32[]{:S(2)}) collective-permute-start(bf16[512,512]{1,0:T(8,128)(2,1)} %get-tuple-element.56), channel_id=1, source_target_pairs={{0,16},{4,20},{8,24},{12,28},{16,0},{20,4},{24,8},{28,12},{1,17},{... | collective-permute-start | bytes 1572872 | tf_op jit(solution)/shard_map/ppermute | solution.py:69
  184.5 20.1 %collective-permute-start.54 = (bf16[128,2048]{1,0:T(8,128)(2,1)}, bf16[128,2048]{1,0:T(8,128)(2,1)S(1)}, u32[]{:S(2)}, u32[]{:S(2)}) collective-permute-start(bf16[128,2048]{1,0:T(8,128)(2,1)} %get-tuple-element.54), channel_id=1, source_target_pairs={{0,8},{4,12},{8,0},{12,4},{16,24},{20,28},{24,16},{28,20},{1,9},{5... | collective-permute-start | bytes 1572872 | tf_op jit(solution)/shard_map/ppermute | solution.py:69
  195.7 58.0 %collective-permute-start.64 = (bf16[128,2048]{1,0:T(8,128)(2,1)S(1)}, bf16[128,2048]{1,0:T(8,128)(2,1)S(1)}, u32[]{:S(2)}, u32[]{:S(2)}) collective-permute-start(bf16[128,2048]{1,0:T(8,128)(2,1)S(1)} %get-tuple-element.55), channel_id=1, source_target_pairs={{0,4},{4,0},{8,12},{12,8},{16,20},{20,16},{24,28},{28,24},{1,5},{5... | collective-permute-start | bytes 1572872 | tf_op jit(solution)/shard_map/ppermute | solution.py:69
  204.6 72.8 %collective-permute-start.57 = (bf16[128,2048]{1,0:T(8,128)(2,1)}, bf16[128,2048]{1,0:T(8,128)(2,1)}, u32[]{:S(2)}, u32[]{:S(2)}) collective-permute-start(bf16[128,2048]{1,0:T(8,128)(2,1)} %get-tuple-element.54), channel_id=1, source_target_pairs={{0,4},{4,0},{8,12},{12,8},{16,20},{20,16},{24,28},{28,24},{1,5},{5... | collective-permute-start | bytes 1572872 | tf_op jit(solution)/shard_map/ppermute | solution.py:69
  221.1 73.4 %collective-permute-start.81 = (bf16[512,512]{1,0:T(8,128)(2,1)}, bf16[512,512]{1,0:T(8,128)(2,1)}, u32[]{:S(2)}, u32[]{:S(2)}) collective-permute-start(bf16[512,512]{1,0:T(8,128)(2,1)} %get-tuple-element.57), channel_id=1, source_target_pairs={{0,4},{4,0},{8,12},{12,8},{16,20},{20,16},{24,28},{28,24},{1,5},{5... | collective-permute-start | bytes 1572872 | tf_op jit(solution)/shard_map/ppermute | solution.py:69
  239.9 67.6 %collective-permute-start.74 = (bf16[512,512]{1,0:T(8,128)(2,1)}, bf16[512,512]{1,0:T(8,128)(2,1)}, u32[]{:S(2)}, u32[]{:S(2)}) collective-permute-start(bf16[512,512]{1,0:T(8,128)(2,1)} %get-tuple-element.56), channel_id=1, source_target_pairs={{0,4},{4,0},{8,12},{12,8},{16,20},{20,16},{24,28},{28,24},{1,5},{5... | collective-permute-start | bytes 1572872 | tf_op jit(solution)/shard_map/ppermute | solution.py:69
  260.9 363.5 %reduce-scatter.2.cloned.1.call-start = ((), (), s32[]{:S(2)}) async-start(), calls=%async_computation.2 | async-start | bytes 5242880 | tf_op jit(solution)/shard_map/reduce_scatter | solution.py:326
  263.6 17.2 %collective-permute-start.58 = (bf16[128,2048]{1,0:T(8,128)(2,1)}, bf16[128,2048]{1,0:T(8,128)(2,1)S(1)}, u32[]{:S(2)}, u32[]{:S(2)}) collective-permute-start(bf16[128,2048]{1,0:T(8,128)(2,1)} %copy-done.46), channel_id=1, source_target_pairs={{0,4},{4,0},{8,12},{12,8},{16,20},{20,16},{24,28},{28,24},{1,5},{5... | collective-permute-start | bytes 1572872 | tf_op jit(solution)/shard_map/ppermute | solution.py:69
  281.9 15.8 %collective-permute-start.83 = (bf16[512,512]{1,0:T(8,128)(2,1)S(1)}, bf16[512,512]{1,0:T(8,128)(2,1)S(1)}, u32[]{:S(2)}, u32[]{:S(2)}) collective-permute-start(bf16[512,512]{1,0:T(8,128)(2,1)S(1)} %copy-done.43), channel_id=1, source_target_pairs={{0,4},{4,0},{8,12},{12,8},{16,20},{20,16},{24,28},{28,24},{1,5},{5... | collective-permute-start | bytes 1572872 | tf_op jit(solution)/shard_map/ppermute | solution.py:69
  297.7 18.2 %collective-permute-start.67 = (bf16[128,2048]{1,0:T(8,128)(2,1)}, bf16[128,2048]{1,0:T(8,128)(2,1)}, u32[]{:S(2)}, u32[]{:S(2)}) collective-permute-start(bf16[128,2048]{1,0:T(8,128)(2,1)} %collective-permute-done.63), channel_id=1, source_target_pairs={{0,4},{4,0},{8,12},{12,8},{16,20},{20,16},{24,28},{28,24},{1,5},{5... | collective-permute-start | bytes 1572872 | tf_op jit(solution)/shard_map/ppermute | solution.py:69
  429.7 42.8 %collective-permute-start.101 = (bf16[2,2,128,1024]{3,2,1,0:T(8,128)(2,1)}, bf16[2,2,128,1024]{3,2,1,0:T(8,128)(2,1)}, u32[]{:S(2)}, u32[]{:S(2)}) collective-permute-start(bf16[2,2,128,1024]{3,2,1,0:T(8,128)(2,1)} %fusion.65), channel_id=1, source_target_pairs={{0,4},{4,0},{8,12},{12,8},{16,20},{20,16},{24,28},{28,24},{1,5},{5... | collective-permute-start | bytes 3145736 | tf_op jit(solution)/shard_map/ppermute | solution.py:69
  434.8 73.9 %collective-permute-start.109 = (bf16[2,2,128,4096]{3,2,1,0:T(8,128)(2,1)}, bf16[2,2,128,4096]{3,2,1,0:T(8,128)(2,1)}, u32[]{:S(2)}, u32[]{:S(2)}) collective-permute-start(bf16[2,2,128,4096]{3,2,1,0:T(8,128)(2,1)} %fusion.21), channel_id=1, source_target_pairs={{0,4},{4,0},{8,12},{12,8},{16,20},{20,16},{24,28},{28,24},{1,5},{5... | collective-permute-start | bytes 12582920 | tf_op jit(solution)/shard_map/ppermute | solution.py:69
  444.6 52.5 %collective-permute-start.117 = (bf16[2,2,512,1024]{3,2,1,0:T(8,128)(2,1)}, bf16[2,2,512,1024]{3,2,1,0:T(8,128)(2,1)}, u32[]{:S(2)}, u32[]{:S(2)}) collective-permute-start(bf16[2,2,512,1024]{3,2,1,0:T(8,128)(2,1)} %fusion.22), channel_id=1, source_target_pairs={{0,4},{4,0},{8,12},{12,8},{16,20},{20,16},{24,28},{28,24},{1,5},{5... | collective-permute-start | bytes 12582920 | tf_op jit(solution)/shard_map/ppermute | solution.py:69
  496.1 86.0 %collective-permute-start.108 = (bf16[32,1024]{1,0:T(8,128)(2,1)S(1)}, bf16[32,1024]{1,0:T(8,128)(2,1)S(1)}, u32[]{:S(2)}, u32[]{:S(2)}) collective-permute-start(bf16[32,1024]{1,0:T(8,128)(2,1)S(1)} %get-tuple-element.66), channel_id=1, source_target_pairs={{0,3},{1,2},{2,1},{3,0},{4,7},{5,6},{6,5},{7,4},{8,11},{9,10},{10,... | collective-permute-start | bytes 196616 | tf_op jit(solution)/shard_map/ppermute | solution.py:69
  497.0 85.2 %collective-permute-start.107 = (bf16[32,1024]{1,0:T(8,128)(2,1)S(1)}, bf16[32,1024]{1,0:T(8,128)(2,1)S(1)}, u32[]{:S(2)}, u32[]{:S(2)}) collective-permute-start(bf16[32,1024]{1,0:T(8,128)(2,1)S(1)} %get-tuple-element.67), channel_id=1, source_target_pairs={{0,2},{1,3},{2,0},{3,1},{4,6},{5,7},{6,4},{7,5},{8,10},{9,11},{10,... | collective-permute-start | bytes 196616 | tf_op jit(solution)/shard_map/ppermute | solution.py:69
  505.6 26.3 %collective-permute-start.120 = (bf16[2,512,512]{2,1,0:T(8,128)(2,1)}, bf16[2,512,512]{2,1,0:T(8,128)(2,1)}, u32[]{:S(2)}, u32[]{:S(2)}) collective-permute-start(bf16[2,512,512]{2,1,0:T(8,128)(2,1)} %fusion.67), channel_id=1, source_target_pairs={{0,16},{4,20},{8,24},{12,28},{16,0},{20,4},{24,8},{28,12},{1,17},{... | collective-permute-start | bytes 3145736 | tf_op jit(solution)/shard_map/ppermute | solution.py:69
  507.3 27.9 %collective-permute-start.118 = (bf16[2,512,512]{2,1,0:T(8,128)(2,1)}, bf16[2,512,512]{2,1,0:T(8,128)(2,1)}, u32[]{:S(2)}, u32[]{:S(2)}) collective-permute-start(bf16[2,512,512]{2,1,0:T(8,128)(2,1)} %fusion.69), channel_id=1, source_target_pairs={{0,8},{4,12},{8,0},{12,4},{16,24},{20,28},{24,16},{28,20},{1,9},{5... | collective-permute-start | bytes 3145736 | tf_op jit(solution)/shard_map/ppermute | solution.py:69
  519.2 31.9 %collective-permute-start.112 = (bf16[2,128,2048]{2,1,0:T(8,128)(2,1)S(1)}, bf16[2,128,2048]{2,1,0:T(8,128)(2,1)S(1)}, u32[]{:S(2)}, u32[]{:S(2)}) collective-permute-start(bf16[2,128,2048]{2,1,0:T(8,128)(2,1)S(1)} %fusion.66), channel_id=1, source_target_pairs={{0,16},{4,20},{8,24},{12,28},{16,0},{20,4},{24,8},{28,12},{1,17},{... | collective-permute-start | bytes 3145736 | tf_op jit(solution)/shard_map/ppermute | solution.py:69
  531.9 22.3 %collective-permute-start.110 = (bf16[2,128,2048]{2,1,0:T(8,128)(2,1)S(1)}, bf16[2,128,2048]{2,1,0:T(8,128)(2,1)S(1)}, u32[]{:S(2)}, u32[]{:S(2)}) collective-permute-start(bf16[2,128,2048]{2,1,0:T(8,128)(2,1)S(1)} %fusion.68), channel_id=1, source_target_pairs={{0,8},{4,12},{8,0},{12,4},{16,24},{20,28},{24,16},{28,20},{1,9},{5... | collective-permute-start | bytes 3145736 | tf_op jit(solution)/shard_map/ppermute | solution.py:69
  535.2 49.6 %collective-permute-start.106 = (bf16[32,1024]{1,0:T(8,128)(2,1)S(1)}, bf16[32,1024]{1,0:T(8,128)(2,1)S(1)}, u32[]{:S(2)}, u32[]{:S(2)}) collective-permute-start(bf16[32,1024]{1,0:T(8,128)(2,1)S(1)} %get-tuple-element.65), channel_id=1, source_target_pairs={{0,1},{1,0},{2,3},{3,2},{4,5},{5,4},{6,7},{7,6},{8,9},{9,8},{10,11... | collective-permute-start | bytes 196616 | tf_op jit(solution)/shard_map/ppermute | solution.py:69
  580.3 32.1 %collective-permute-start.123 = (bf16[128,1024]{1,0:T(8,128)(2,1)S(1)}, bf16[128,1024]{1,0:T(8,128)(2,1)S(1)}, u32[]{:S(2)}, u32[]{:S(2)}) collective-permute-start(bf16[128,1024]{1,0:T(8,128)(2,1)S(1)} %get-tuple-element.50), channel_id=1, source_target_pairs={{0,2},{1,3},{2,0},{3,1},{4,6},{5,7},{6,4},{7,5},{8,10},{9,11},{10,... | collective-permute-start | bytes 786440 | tf_op jit(solution)/shard_map/ppermute | solution.py:69
  582.1 30.3 %collective-permute-start.122 = (bf16[128,1024]{1,0:T(8,128)(2,1)S(1)}, bf16[128,1024]{1,0:T(8,128)(2,1)S(1)}, u32[]{:S(2)}, u32[]{:S(2)}) collective-permute-start(bf16[128,1024]{1,0:T(8,128)(2,1)S(1)} %get-tuple-element.48), channel_id=1, source_target_pairs={{0,1},{1,0},{2,3},{3,2},{4,5},{5,4},{6,7},{7,6},{8,9},{9,8},{10,11... | collective-permute-start | bytes 786440 | tf_op jit(solution)/shard_map/ppermute | solution.py:69
  582.1 31.2 %collective-permute-start.116 = (bf16[32,4096]{1,0:T(8,128)(2,1)S(1)}, bf16[32,4096]{1,0:T(8,128)(2,1)S(1)}, u32[]{:S(2)}, u32[]{:S(2)}) collective-permute-start(bf16[32,4096]{1,0:T(8,128)(2,1)S(1)} %get-tuple-element.52), channel_id=1, source_target_pairs={{0,3},{1,2},{2,1},{3,0},{4,7},{5,6},{6,5},{7,4},{8,11},{9,10},{10,... | collective-permute-start | bytes 786440 | tf_op jit(solution)/shard_map/ppermute | solution.py:69
  584.8 38.7 %collective-permute-start.115 = (bf16[32,4096]{1,0:T(8,128)(2,1)S(1)}, bf16[32,4096]{1,0:T(8,128)(2,1)S(1)}, u32[]{:S(2)}, u32[]{:S(2)}) collective-permute-start(bf16[32,4096]{1,0:T(8,128)(2,1)S(1)} %get-tuple-element.53), channel_id=1, source_target_pairs={{0,2},{1,3},{2,0},{3,1},{4,6},{5,7},{6,4},{7,5},{8,10},{9,11},{10,... | collective-permute-start | bytes 786440 | tf_op jit(solution)/shard_map/ppermute | solution.py:69
  588.3 35.2 %collective-permute-start.114 = (bf16[32,4096]{1,0:T(8,128)(2,1)S(1)}, bf16[32,4096]{1,0:T(8,128)(2,1)S(1)}, u32[]{:S(2)}, u32[]{:S(2)}) collective-permute-start(bf16[32,4096]{1,0:T(8,128)(2,1)S(1)} %get-tuple-element.51), channel_id=1, source_target_pairs={{0,1},{1,0},{2,3},{3,2},{4,5},{5,4},{6,7},{7,6},{8,9},{9,8},{10,11... | collective-permute-start | bytes 786440 | tf_op jit(solution)/shard_map/ppermute | solution.py:69
  643.9 35.5 %collective-permute-start.93 = (bf16[2,2,128,3072]{3,2,1,0:T(8,128)(2,1)}, bf16[2,2,128,3072]{3,2,1,0:T(8,128)(2,1)}, u32[]{:S(2)}, u32[]{:S(2)}) collective-permute-start(bf16[2,2,128,3072]{3,2,1,0:T(8,128)(2,1)} %fusion.28), channel_id=1, source_target_pairs={{0,4},{4,0},{8,12},{12,8},{16,20},{20,16},{24,28},{28,24},{1,5},{5... | collective-permute-start | bytes 9437192 | tf_op jit(solution)/shard_map/ppermute | solution.py:69
  686.8 16.3 %collective-permute-start.94 = (bf16[2,128,1536]{2,1,0:T(8,128)(2,1)S(1)}, bf16[2,128,1536]{2,1,0:T(8,128)(2,1)S(1)}, u32[]{:S(2)}, u32[]{:S(2)}) collective-permute-start(bf16[2,128,1536]{2,1,0:T(8,128)(2,1)S(1)} %fusion.75), channel_id=1, source_target_pairs={{0,8},{4,12},{8,0},{12,4},{16,24},{20,28},{24,16},{28,20},{1,9},{5... | collective-permute-start | bytes 2359304 | tf_op jit(solution)/shard_map/ppermute | solution.py:69
  (152 other events, 1992.1 us)
Sparse Core Ops, SparseCore 0:
  261.1 81.2 all-gather.1
  480.0 78.5 reduce-scatter.1

commit v2 on v0

v2 whole, which is shorter than its diff:
```python
import jax
import jax.numpy as jnp
from jax import lax
from jax.experimental import pallas as pl
from jax.experimental.pallas import tpu as pltpu
from jax.sharding import PartitionSpec as P

HEAD_DIM = 64
PIECE = 256


gelu_scale = 0.7978845608028654
gelu_cubic = 0.044715


def layer_norm_parts(rows_in, gain, shift):
    mean_row = jnp.mean(rows_in, axis=-1, keepdims=True)
    centered = rows_in - mean_row
    inverse = lax.rsqrt(jnp.mean(centered * centered, axis=-1, keepdims=True) + 1e-05)
    unit_rows = centered * inverse
    return (unit_rows * gain + shift, unit_rows, inverse)


def layer_norm_back(grad_in, unit_rows, inverse, gain):
    scaled = grad_in * gain
    back_rows = inverse * (
        scaled
        - jnp.mean(scaled, axis=-1, keepdims=True)
        - unit_rows * jnp.mean(scaled * unit_rows, axis=-1, keepdims=True)
    )
    return (back_rows, jnp.sum(grad_in * unit_rows, axis=0), jnp.sum(grad_in, axis=0))


def gelu_parts(values):
    tangent = jnp.tanh(gelu_scale * (values + gelu_cubic * values * values * values))
    slope = 0.5 * (1.0 + tangent) + 0.5 * values * (1.0 - tangent * tangent) * gelu_scale * (
        1.0 + 3.0 * gelu_cubic * values * values
    )
    return (0.5 * values * (1.0 + tangent), slope)


def piece_labels(positions, starts):
    inside = (positions[:, :, None] >= starts[:, None, :]) & (
        positions[:, :, None] < starts[:, None, :] + PIECE
    )
    labels = jnp.arange(1, starts.shape[1] + 1, dtype=jnp.int32)
    return jnp.sum(jnp.where(inside, labels[None, None, :], 0), axis=2)


def visible(query_at, key_at, query_seg, key_seg, query_piece, key_piece, valid):
    query_pos = query_at[None, :, None]
    key_pos = key_at[None, None, :]
    limit_len = valid[:, None, None]
    same_seg = query_seg[:, :, None] == key_seg[:, None, :]
    together = (query_piece[:, :, None] == key_piece[:, None, :]) & (query_piece[:, :, None] > 0)
    rule_ok = same_seg & ((key_pos <= query_pos) | together)
    return (key_pos < limit_len) & ((query_pos >= limit_len) | rule_ok)


def swap(value, axis, bit, size):
    return lax.ppermute(value, axis, [(i, i ^ bit) for i in range(size)])


def doubled(bits):
    order = [0]
    for bit in bits:
        order = order + [at ^ bit for at in order]
    return order


def far_bits(dp_size):
    bits = [1 << i for i in range(1, dp_size.bit_length() - 1)]
    half = (len(bits) + 1) // 2
    return bits, bits[half:] + bits[:half]


def add(left, right):
    return (left.astype(jnp.float32) + right.astype(jnp.float32)).astype(left.dtype)


def by_place(blocks, me):
    out, bit = list(blocks), 1
    while bit < len(out):
        odd = jnp.bitwise_and(me, bit) > 0
        out = [jnp.where(odd, out[i ^ bit], out[i]) for i in range(len(out))]
        bit *= 2
    return out


def pick_columns_body(index_ref, in_ref, out_ref):
    width = out_ref.shape[1] // index_ref.shape[0]
    for i in range(index_ref.shape[0]):
        at = pl.multiple_of(index_ref[i] * width, width)
        out_ref[:, i * width : (i + 1) * width] = in_ref[:, pl.ds(at, width)]


def pick_columns(rows, index, count):
    width = rows.shape[1] // count
    if width % 128:
        parts = [lax.dynamic_slice_in_dim(rows, index[i] * width, width, 1) for i in range(count)]
        return jnp.concatenate(parts, axis=1)
    return pl.pallas_call(
        pick_columns_body,
        out_shape=jax.ShapeDtypeStruct(rows.shape, rows.dtype),
        in_specs=[
            pl.BlockSpec(memory_space=pltpu.SMEM),
            pl.BlockSpec(memory_space=pltpu.VMEM),
        ],
        out_specs=pl.BlockSpec(memory_space=pltpu.VMEM),
        name="pick_columns",
    )(index, rows)


def pick_rows(table, index):
    chosen = index[:, None] == jnp.arange(table.shape[0], dtype=jnp.int32)[None, :]
    return jnp.sum(jnp.where(chosen[:, :, None], table[None], 0.0), axis=1)


def after(value, *earlier):
    return lax.optimization_barrier((value,) + earlier)[0]


def spread(piece, dp_size, split):
    rows = piece.shape[0]
    bits_x, bits_y = far_bits(dp_size)
    order = doubled(bits_x)
    parts = [(piece, bits_x)]
    if split:
        parts = [(piece[: rows // 2], bits_x), (piece[rows // 2 :], bits_y)]
    bufs = [part for part, _ in parts]
    for step in range(len(bits_x)):
        got = [swap(buf, "dp", bits[step], dp_size) for buf, (_, bits) in zip(bufs, parts)]
        bufs = [jnp.concatenate(pair, axis=0) for pair in zip(bufs, got)]
    if split:
        half, order_y = rows // 2, doubled(bits_y)
        slices = []
        for at in order:
            for buf, places in zip(bufs, (order, order_y)):
                i = places.index(at)
                slices.append(buf[i * half : (i + 1) * half])
        own = jnp.concatenate(slices, axis=0)
    else:
        own = bufs[0]
    return own, swap(own, "dp", 1, dp_size)


def collect(own, odd, dp_size, split):
    bits_x, bits_y = far_bits(dp_size)
    order, count = doubled(bits_x), dp_size // 2
    got = [swap(part, "dp", 1, dp_size) for part in odd]
    stacks = [
        (a.reshape(count, -1, a.shape[1]), b.reshape(count, -1, a.shape[1]))
        for a, b in zip(own, got)
    ]
    rows = stacks[0][0].shape[1]

    def taken(which, low, high):
        cols = [
            jnp.concatenate([add(a[i, low:high], b[i, low:high]) for a, b in stacks], axis=1)
            for i in which
        ]
        return jnp.stack(cols)

    plans = [(bits_x, 0, rows)]
    if split:
        plans = [(bits_x, 0, rows // 2), (bits_y, rows // 2, rows)]
    keeps = []
    half = count // 2
    for bits, low, high in plans:
        places = [order.index(at) for at in doubled(bits)]
        keeps.append((taken(places[:half], low, high), taken(places[half:], low, high)))
    for step in reversed(range(len(bits_x))):
        got = [swap(send, "dp", bits[step], dp_size) for (_, send), (bits, _, _) in zip(keeps, plans)]
        if step:
            cut = (1 << step) // 2
            keeps = [
                (add(keep[:cut], new[:cut]), add(keep[cut:], new[cut:]))
                for (keep, _), new in zip(keeps, got)
            ]
        else:
            keeps = [add(keep, new)[0] for (keep, _), new in zip(keeps, got)]
    return jnp.concatenate(keeps, axis=0)


def seq_gather(shard, seq_size, earlier=()):
    out = [shard]
    for k in range(1, seq_size):
        out.append(swap(after(shard, earlier[k]) if earlier else shard, "seq", k, seq_size))
    return out


def seq_sum(piece, seq_size, seq_at):
    rows = piece.shape[0] // seq_size
    cut = lambda k: lax.dynamic_slice_in_dim(piece, jnp.bitwise_xor(seq_at, k) * rows, rows, 0)
    total = cut(0).astype(jnp.float32)
    for k in range(1, seq_size):
        total = total + swap(cut(k), "seq", k, seq_size).astype(jnp.float32)
    return total


def sum_all(value, dp_size, seq_size):
    bit = 1
    while bit < dp_size:
        value = value + swap(value, "dp", bit, dp_size)
        bit *= 2
    bit = 1
    while bit < seq_size:
        value = value + swap(value, "seq", bit, seq_size)
        bit *= 2
    return value


def dot(left, right):
    return jnp.dot(left, right, preferred_element_type=jnp.float32)


def dot_back(grad, weight):
    return jnp.einsum("rn,kn->rk", grad, weight, preferred_element_type=jnp.float32)


def dot_rows(rows, grad):
    return jnp.einsum("rk,rn->kn", rows, grad, preferred_element_type=jnp.float32)


def apply(rows, pair):
    half = rows.shape[1] // 2
    return dot(rows[:, :half], pair[0]) + dot(rows[:, half:], pair[1])


def apply_back(grad, pair, dtype=jnp.float32):
    return jnp.concatenate([dot_back(grad, part).astype(dtype) for part in pair], axis=1)


def weight_grads(rows, grad):
    half = rows.shape[1] // 2
    return [dot_rows(part, grad).astype(jnp.bfloat16) for part in (rows[:, :half], rows[:, half:])]


def heads_of(rows):
    return rows.reshape(rows.shape[0], -1, HEAD_DIM).transpose(1, 0, 2)


def rows_of(stacked):
    return stacked.transpose(1, 0, 2).reshape(stacked.shape[1], -1)


def per_device(
    tokens,
    cotangent,
    valid_length,
    segment_ids,
    piece_starts,
    norm1_gain,
    norm1_bias,
    qkv_weight,
    qv_bias,
    out_weight,
    out_bias,
    norm2_gain,
    norm2_bias,
    up_weight,
    up_bias,
    down_weight,
    down_bias,
):
    f32, bf16 = jnp.float32, jnp.bfloat16
    _, local_len, width = tokens.shape
    score_scale = HEAD_DIM ** (-0.5)
    dp_size, seq_size = lax.axis_size("dp"), lax.axis_size("seq")
    dp_at, seq_at = lax.axis_index("dp"), lax.axis_index("seq")
    devices = dp_size * seq_size
    group = width // seq_size

    half_order = doubled(far_bits(dp_size)[0])
    full = half_order + [at ^ 1 for at in half_order]
    back = [full.index(at) for at in range(dp_size)]
    full_at = jnp.array(full, jnp.int32)
    to_x = jnp.bitwise_xor(dp_at, full_at)
    natural = jnp.arange(dp_size, dtype=jnp.int32)
    place_in_x = lambda block: jnp.sum(
        jnp.where(
            jnp.bitwise_xor(dp_at, block)[:, None] == natural[None, :],
            jnp.array(back, jnp.int32)[None, :],
            0,
        ),
        axis=1,
    )
    from_x = place_in_x(natural)
    per_group = dp_size // seq_size
    in_groups = lambda block: jnp.bitwise_xor(seq_at, block // per_group) * per_group + block % per_group
    groups_to_x = in_groups(to_x)
    x_to_groups = place_in_x(in_groups(natural))

    vectors = (norm1_gain, norm1_bias, qv_bias, out_bias, norm2_gain, norm2_bias, up_bias, down_bias)
    widths = [v.shape[0] for v in vectors]
    rows_one = qkv_weight.shape[0]
    packed = jnp.concatenate(vectors)
    vec_rows = -(-packed.shape[0] // 128)
    vec_block = jnp.pad(packed, (0, rows_one * 128 - packed.shape[0])).reshape(rows_one, 128)
    qkv_split = qkv_weight.reshape(rows_one, 3, seq_size, group)

    def qkv_part(k):
        mine = lax.dynamic_index_in_dim(qkv_split, jnp.bitwise_xor(seq_at, k), 2, keepdims=False)
        return jnp.concatenate([mine.reshape(rows_one, 3 * group), vec_block], axis=1)

    own_x = pick_columns(tokens[0], to_x, dp_size)
    first = [qkv_part(0)] + [swap(qkv_part(k), "seq", k, seq_size) for k in range(1, seq_size)]
    second = seq_gather(jnp.concatenate([out_weight, up_weight], axis=1), seq_size)
    token_blocks = seq_gather(own_x, seq_size, second)
    third = seq_gather(down_weight, seq_size, token_blocks)
    stacked = lambda blocks: jnp.concatenate(by_place(blocks, seq_at), axis=0)
    one_pair = spread(stacked(first), dp_size, False)
    two_pair = spread(stacked(second), dp_size, True)
    down_pair = spread(stacked(third), dp_size, True)
    qkv_pair = [part[:, : 3 * group] for part in one_pair]
    out_pair = [part[:, :width] for part in two_pair]
    up_pair = [part[:, width:] for part in two_pair]

    vec_x = jnp.concatenate([part[:, 3 * group :] for part in one_pair], axis=0).astype(f32)
    vec_x = vec_x.reshape(dp_size, seq_size, rows_one, 128)[:, :, :vec_rows]
    vec_x = vec_x.reshape(dp_size, seq_size, vec_rows * 128)
    vec_n = pick_rows(vec_x.reshape(dp_size, -1), from_x).reshape(vec_x.shape)

    def field(table, which):
        at = sum(widths[:which])
        return table[:, :, at : at + widths[which]].reshape(-1)

    gain_one, shift_one, gain_two, shift_two = [field(vec_x, i) for i in (0, 1, 4, 5)]
    qv_full, out_shift, up_shift, down_shift = [field(vec_n, i) for i in (2, 3, 6, 7)]

    starts = [jnp.bitwise_xor(seq_at, k) * local_len for k in range(seq_size)]
    step = jnp.arange(local_len, dtype=jnp.int32)
    place = jnp.concatenate([at + step for at in starts])
    segments = jnp.concatenate(
        [lax.dynamic_slice_in_dim(segment_ids, at, local_len, 1) for at in starts], axis=1
    )
    pieces = piece_labels(place[None, :], piece_starts)
    allowed = visible(place, place, segments, segments, pieces, pieces, valid_length)
    live_rows = (starts[0] + step < valid_length[0]).astype(f32)[:, None]

    all_x = jnp.concatenate(token_blocks, axis=0).astype(f32)
    normed_one = layer_norm_parts(all_x, gain_one, shift_one)[0].astype(bf16)
    half_bias = qv_full.reshape(2, seq_size, group)
    half_bias = lax.dynamic_index_in_dim(half_bias, seq_at, 1, keepdims=False)
    qkv_shift = jnp.concatenate([half_bias[0], jnp.zeros((group,), f32), half_bias[1]])
    qkv_rows = (apply(normed_one, qkv_pair) + qkv_shift).astype(bf16)
    query_heads, key_heads, value_heads = [
        heads_of(qkv_rows[:, i * group : (i + 1) * group]) for i in range(3)
    ]
    raw = (
        jnp.einsum("hqd,hkd->hqk", query_heads, key_heads, preferred_element_type=f32) * score_scale
    )
    row_top = jnp.max(jnp.where(allowed, raw, -1e30), axis=-1, keepdims=True)
    expo = jnp.exp(jnp.where(allowed, raw - row_top, -1e30))
    row_total = jnp.sum(expo, axis=-1, keepdims=True)
    attn_probs = (expo / row_total).astype(bf16)
    head_out = jnp.einsum("hqk,hkd->hqd", attn_probs, value_heads, preferred_element_type=f32)
    lse_all = row_top + jnp.log(row_total)
    attended_rows = rows_of(head_out.astype(bf16))

    cut_rows = lambda rows, k: rows[k * local_len : (k + 1) * local_len]
    attended = [cut_rows(attended_rows, 0)] + [
        swap(cut_rows(attended_rows, k), "seq", k, seq_size) for k in range(1, seq_size)
    ]
    attended = pick_columns(jnp.concatenate(attended, axis=1), groups_to_x, dp_size)
    branch = apply(attended, out_pair) + out_shift
    tokens_f = tokens[0].astype(f32)
    middle = tokens_f + branch
    middle_x = pick_columns(middle, to_x, dp_size)
    normed_two, unit_two, inverse_two = layer_norm_parts(middle_x, gain_two, shift_two)
    normed_two = normed_two.astype(bf16)
    hidden = pick_columns(apply(normed_two, up_pair) + up_shift, to_x, dp_size)
    gelu_value, gelu_slope = gelu_parts(hidden)
    gated = gelu_value.astype(bf16)
    mlp_out = apply(gated, down_pair) + down_shift
    result = middle + mlp_out
    output = result.astype(bf16)[None]
    squares = jnp.stack(
        [
            jnp.sum(live_rows * entry * entry)
            for entry in (tokens_f, branch, middle, mlp_out, result)
        ]
    )
    counted = jnp.concatenate([squares, jnp.sum(live_rows)[None]])
    counted = sum_all(jnp.pad(counted, (0, 122))[None], dp_size, seq_size)[0]
    residual_rms = jnp.sqrt(counted[:5] / (counted[5] * width))

    grad_out = cotangent[0] * live_rows.astype(bf16)
    down_grads = weight_grads(gated, grad_out)
    down_piece = collect([down_grads[0]], [down_grads[1]], dp_size, True)
    grad_hidden = (apply_back(grad_out, down_pair) * gelu_slope).astype(bf16)
    grad_hidden = pick_columns(grad_hidden, from_x, dp_size)
    up_grads = weight_grads(normed_two, grad_hidden)
    grad_normed_two = apply_back(grad_hidden, up_pair)
    grad_mid_norm, grad_norm2_gain, grad_norm2_bias = layer_norm_back(
        grad_normed_two, unit_two, inverse_two, gain_two
    )
    grad_middle = grad_out.astype(f32) + pick_columns(grad_mid_norm, from_x, dp_size)
    grad_branch = grad_middle.astype(bf16)
    out_grads = weight_grads(attended, grad_branch)
    grad_attended = pick_columns(apply_back(grad_branch, out_pair, bf16), x_to_groups, dp_size)
    two_piece = collect(
        [out_grads[0], up_grads[0]], [out_grads[1], up_grads[1]], dp_size, True
    )
    cut_cols = lambda rows, k: rows[:, k * group : (k + 1) * group]
    grad_heads = heads_of(
        jnp.concatenate(
            [cut_cols(grad_attended, 0)]
            + [swap(cut_cols(grad_attended, k), "seq", k, seq_size) for k in range(1, seq_size)],
            axis=0,
        )
    )
    raw = (
        jnp.einsum("hqd,hkd->hqk", query_heads, key_heads, preferred_element_type=f32) * score_scale
    )
    attn_probs = jnp.exp(jnp.where(allowed, raw - lse_all, -1e30))
    grad_probs = jnp.einsum("hqd,hkd->hqk", grad_heads, value_heads, preferred_element_type=f32)
    inner_sum = jnp.sum(attn_probs * grad_probs, axis=-1, keepdims=True)
    grad_scores = (attn_probs * (grad_probs - inner_sum)).astype(bf16)
    grad_query = (
        jnp.einsum("hqk,hkd->hqd", grad_scores, key_heads, preferred_element_type=f32) * score_scale
    )
    grad_key = (
        jnp.einsum("hqk,hqd->hkd", grad_scores, query_heads, preferred_element_type=f32)
        * score_scale
    )
    grad_value = jnp.einsum(
        "hqk,hqd->hkd", attn_probs.astype(bf16), grad_heads, preferred_element_type=f32
    )
    grad_qkv = jnp.concatenate(
        [rows_of(part.astype(bf16)) for part in (grad_query, grad_key, grad_value)], axis=1
    )
    part_normed = apply_back(grad_qkv, qkv_pair, bf16)
    grad_normed_one = cut_rows(part_normed, 0).astype(f32)
    for k in range(1, seq_size):
        grad_normed_one = grad_normed_one + swap(
            cut_rows(part_normed, k), "seq", k, seq_size
        ).astype(f32)
    unit_one, inverse_one = layer_norm_parts(own_x.astype(f32), gain_one, shift_one)[1:]
    grad_in_norm, grad_norm1_gain, grad_norm1_bias = layer_norm_back(
        grad_normed_one, unit_one, inverse_one, gain_one
    )
    tokens_grad = (grad_middle + pick_columns(grad_in_norm, from_x, dp_size)).astype(bf16)[None]

    column_sums = jnp.sum(grad_qkv.astype(f32), axis=0).reshape(3, 1, group)
    grad_qv_bias = lax.dynamic_update_slice(
        jnp.zeros((2, seq_size, group), f32),
        jnp.concatenate([column_sums[:1], column_sums[2:]], axis=0),
        (0, seq_at, 0),
    )
    grad_out_bias = jnp.sum(grad_branch.astype(f32), axis=0)
    grad_up_bias = jnp.sum(grad_hidden.astype(f32), axis=0)
    grad_down_bias = jnp.sum(grad_out.astype(f32), axis=0)
    by_device = lambda v: v.reshape(dp_size, seq_size, -1)
    plain = [by_device(v) for v in (grad_qv_bias, grad_out_bias, grad_up_bias, grad_down_bias)]
    plain_widths = [v.shape[2] for v in plain]
    plain_x = pick_rows(jnp.concatenate(plain, axis=2).reshape(dp_size, -1), to_x)
    plain_x = plain_x.reshape(dp_size, seq_size, -1)
    cuts, at = [], 0
    for size in plain_widths:
        cuts.append(plain_x[:, :, at : at + size])
        at += size
    moved = [by_device(v) for v in (grad_norm1_gain, grad_norm1_bias, grad_norm2_gain, grad_norm2_bias)]
    vec_grads = jnp.concatenate(
        [moved[0], moved[1], cuts[0], cuts[1], moved[2], moved[3], cuts[2], cuts[3]], axis=2
    ).astype(bf16)
    vec_size = vec_grads.shape[2]
    vec_grads = jnp.pad(vec_grads, ((0, 0), (0, 0), (0, rows_one * 128 - vec_size)))
    vec_grads = vec_grads.reshape(2, -1, 128)
    qkv_grads = weight_grads(normed_one, grad_qkv)
    one_piece = collect(
        [qkv_grads[0], vec_grads[0]], [qkv_grads[1], vec_grads[1]], dp_size, False
    )
    cut_one = lambda k: lax.dynamic_slice_in_dim(
        one_piece, jnp.bitwise_xor(seq_at, k) * rows_one, rows_one, 0
    )
    one_blocks = [cut_one(0)] + [swap(cut_one(k), "seq", k, seq_size) for k in range(1, seq_size)]
    one_blocks = [block.astype(f32) for block in one_blocks]
    qkv_grad = jnp.stack(
        [part.reshape(rows_one, 3, group) for part in by_place([b[:, : 3 * group] for b in one_blocks], seq_at)],
        axis=2,
    ).reshape(rows_one, 3 * width)
    vec_sum = sum(block[:, 3 * group :] for block in one_blocks).reshape(-1)
    small, at = [], 0
    for size in widths:
        small.append(vec_sum[at : at + size])
        at += size
    n1g, n1b, qvb, ob, n2g, n2b, ub, db = small

    down_grad = seq_sum(down_piece, seq_size, seq_at)
    two_grad = seq_sum(two_piece, seq_size, seq_at)
    out_grad, up_grad = two_grad[:, :width], two_grad[:, width:]
    return (
        output,
        tokens_grad,
        n1g,
        n1b,
        qkv_grad,
        qvb,
        out_grad,
        ob,
        n2g,
        n2b,
        up_grad,
        ub,
        down_grad,
        db,
        residual_rms,
    )


def solution(mesh):
    return jax.shard_map(
        per_device,
        mesh=mesh,
        in_specs=(
            P("dp", "seq", None),
            P("dp", "seq", None),
            P("dp"),
            P("dp", None),
            P("dp", None),
            P(("dp", "seq")),
            P(("dp", "seq")),
            P(("dp", "seq"), None),
            P(("dp", "seq")),
            P(("dp", "seq"), None),
            P(("dp", "seq")),
            P(("dp", "seq")),
            P(("dp", "seq")),
            P(("dp", "seq"), None),
            P(("dp", "seq")),
            P(("dp", "seq"), None),
            P(("dp", "seq")),
        ),
        out_specs=(
            P("dp", "seq", None),
            P("dp", "seq", None),
            P(("dp", "seq")),
            P(("dp", "seq")),
            P(("dp", "seq"), None),
            P(("dp", "seq")),
            P(("dp", "seq"), None),
            P(("dp", "seq")),
            P(("dp", "seq")),
            P(("dp", "seq")),
            P(("dp", "seq"), None),
            P(("dp", "seq")),
            P(("dp", "seq"), None),
            P(("dp", "seq")),
            P(),
        ),
        check_vma=False,
    )
```

time: 1580 us -> 598 us (0.38)
  waiting for transfers between devices: 1220 us -> 231 us
  blocking collectives: 154 us -> 0 us
  starting transfers between devices: 0.65 us -> 89.9 us
  other arithmetic: 27.9 us -> 88.8 us
  Pallas kernels: 0 us -> 20.9 us
  local copies, waits for them, and re-layouts: 34.1 us -> 51.4 us
    reduce_scatter x5 -> x0, waiting for transfers between devices: 1010 us -> none  [the longest x1 365 us: per_device(): lax.psum_scatter(grad_up_weight, ('dp', 'seq'), scatter_dimension=0, tile...]
    ppermute x0 -> x63, waiting for transfers between devices: none -> 231 us  [swap(): return lax.ppermute(value, axis, [(i, i ^ bit) for i in range(size)])]
    all_gather x5 -> x0, waiting for transfers between devices: 207 us -> none  [the longest x1 75.1 us: per_device(): lax.all_gather(up_weight, ('dp', 'seq'), axis=0, tiled=True)]
    ppermute x0 -> x63, starting transfers between devices: none -> 89.9 us  [swap(): return lax.ppermute(value, axis, [(i, i ^ bit) for i in range(size)])]
    unnamed x2 -> x0, blocking collectives: 85.2 us -> none
    all_gather x1 -> x0, blocking collectives: 68.7 us -> none  [per_device(): lax.all_gather(up_bias, ('dp', 'seq'), axis=0, tiled=True)]
    pallas_call x0 -> x8, Pallas kernels: none -> 20.9 us  [pick_columns(): pl.pallas_call(pick_columns_body, out_shape=jax.ShapeDtypeStruct(rows.sha...]
    convert_element_type x11 -> x19, other arithmetic: 12.1 us -> 30.7 us  [the longest x1 12.2 us: per_device(): grad_scores = (attn_probs * (grad_probs - inner_sum)).astype(bf16)]
  transfers between devices with their start and end apart: 10 -> 63, of which waited for: 10 -> 27; matrix products, arithmetic and copies ran while one was open for 7% -> 32% of each run, Pallas kernels for 0% -> 2%
where the time goes in v2:
time: 598 us; the launch traced here: 592 us
  waiting for transfers between devices  231 us (39%)
  matrix products  106 us (18%)
  starting transfers between devices  89.9 us (15%)
  other arithmetic  88.8 us (15%)
  local copies, waits for them, and re-layouts  51.4 us (9%)
  Pallas kernels  20.9 us (3%)
    ppermute x63, waiting for transfers between devices, swap(): return lax.ppermute(value, axis, [(i, i ^ bit) for i in range(size)])  231 us
    ppermute x63, starting transfers between devices, swap(): return lax.ppermute(value, axis, [(i, i ^ bit) for i in range(size)])  89.9 us
    dot_general x8, matrix products, dot_back(): jnp.einsum('rn,kn->rk', grad, weight, preferred_element_type=jnp.float32)  25.5 us
    dot_general x8, matrix products, dot(): return jnp.dot(left, right, preferred_element_type=jnp.float32)  24.7 us
    pallas_call x8, Pallas kernels, pick_columns(): pl.pallas_call(pick_columns_body, out_shape=jax.ShapeDtypeStruct(rows.sha...  20.9 us
    unnamed x158, local copies, waits for them, and re-layouts  20 us
    dot_general x8, matrix products, dot_rows(): jnp.einsum('rk,rn->kn', rows, grad, preferred_element_type=jnp.float32)  18.2 us
    convert_element_type x1, other arithmetic, per_device(): grad_scores = (attn_probs * (grad_probs - inner_sum)).astype(bf16)  12.2 us
  transfers between devices with their start and end apart: 63, of which 27 were waited for; matrix products, arithmetic and copies ran while one was open for 32% of the time, Pallas kernels for 2%

profile of v2, /device:TPU:0, one launch (start us, length us, event | category | flops | bytes accessed | tf_op | source)
XLA Modules:
  0.0 591.8 jit_solution(15953306127188510495)
XLA Ops:
  2.5 5.1 collective-permute-start.4
  7.6 5.4 concatenate.221
  33.8 6.1 %collective-permute-done.7 = bf16[32,896]{1,0:T(8,128)(2,1)S(1)} collective-permute-done((bf16[32,896]{1,0:T(8,128)(2,1)S(1)}, bf16[32,896]{1,0:T(8,128)(2,1)S(1)}, u32[]{:S(2)}, u32[]{:S(2)}) %collective-permute-start.7) | collective-permute-done | bytes 57376 | tf_op jit(solution)/shard_map/ppermute | solution.py:61
  41.7 4.5 collective-permute-done.9
  59.3 9.4 %collective-permute-done.1 = bf16[256,1024]{1,0:T(8,128)(2,1)S(1)} collective-permute-done((bf16[256,1024]{1,0:T(8,128)(2,1)S(1)}, bf16[256,1024]{1,0:T(8,128)(2,1)S(1)}, u32[]{:S(2)}, u32[]{:S(2)}) %collective-permute-start.1) | collective-permute-done | bytes 524320 | tf_op jit(solution)/shard_map/ppermute | solution.py:61
  68.7 19.4 %collective-permute-done.3 = bf16[256,1024]{1,0:T(8,128)(2,1)S(1)} collective-permute-done((bf16[256,1024]{1,0:T(8,128)(2,1)S(1)}, bf16[256,1024]{1,0:T(8,128)(2,1)S(1)}, u32[]{:S(2)}, u32[]{:S(2)}) %collective-permute-start.3) | collective-permute-done | bytes 524320 | tf_op jit(solution)/shard_map/ppermute | solution.py:61
  88.2 16.6 %collective-permute-start.21 = (bf16[128,1024]{1,0:T(8,128)(2,1)S(1)}, bf16[128,1024]{1,0:T(8,128)(2,1)S(1)}, u32[]{:S(2)}, u32[]{:S(2)}) collective-permute-start(bf16[128,1024]{1,0:T(8,128)(2,1)S(1)} %copy-done.29), channel_id=1, source_target_pairs={{0,2},{1,3},{2,0},{3,1},{4,6},{5,7},{6,4},{7,5},{8,10},{9,11},{10,... | collective-permute-start | bytes 786440 | tf_op jit(solution)/shard_map/ppermute | solution.py:61
  122.0 28.0 %collective-permute-done.24 = bf16[256,1024]{1,0:T(8,128)(2,1)S(1)} collective-permute-done((bf16[256,1024]{1,0:T(8,128)(2,1)S(1)}, bf16[256,1024]{1,0:T(8,128)(2,1)S(1)}, u32[]{:S(2)}, u32[]{:S(2)}) %collective-permute-start.24) | collective-permute-done | bytes 524320 | tf_op jit(solution)/shard_map/ppermute | solution.py:61
  160.3 3.3 select_reduce_fusion
  163.6 3.2 slice_dynamic-update-slice_fusion.3
  183.5 4.2 fusion
  188.2 8.5 %fusion.40 = bf16[1024,4,64]{0,2,1:T(8,128)(2,1)S(1)} fusion(bf16[4,1024,64]{1,2,0:T(8,128)(2,1)S(1)} %bitcast.188, f32[4,1024,1024]{1,2,0:T(8,128)} %copy-done, f32[4,1024]{1,0:T(4,128)S(1)} %fusion, f32[4,1024]{1,0:T(4,128)S(1)} %get-tuple-element.172, pred[1024,1024]{0,1:T(8,128)(4,1)S(1)} %or_and_fusion), kind=kOutput, calls=%fused_computation.111 | convolution fusion | flops 558104576 | bytes 18907136 | tf_op jit(solution)/shard_map/hqk,hkd->hqd/dot_general | solution.py:357
  201.6 3.1 collective-permute-done.12
  204.7 5.5 collective-permute-done.13
  213.1 4.8 fusion.128
  218.0 4.9 fusion.127
  224.6 3.0 convert_add_fusion.1
  234.3 3.6 fusion.22
  238.0 5.4 fusion.6.in_ref
  243.4 4.6 pick_columns.11
  248.0 6.2 %fusion.19 = (bf16[256,4096]{1,0:T(8,128)(2,1)}, bf16[256,4096]{1,0:T(8,128)(2,1)}) fusion(f32[256,4096]{1,0:T(8,128)} %pick_columns.11, f32[256,2048]{1,0:T(8,128)} %fusion.127, f32[256,2048]{1,0:T(8,128)S(1)} %copy-done.36), kind=kLoop, calls=%fused_computation.31 | loop fusion | flops 23068672 | bytes 12582912 | tf_op jit(solution)/shard_map/convert_element_type | solution.py:391
  254.3 3.1 pick_columns.12
  257.3 5.1 fusion.24
  262.4 3.4 convolution_convert_fusion
  265.8 3.3 convolution_convert_fusion.1
  269.0 3.4 convolution_convert_fusion.2
  272.4 3.6 fusion.52
  276.1 5.2 fusion.50
  281.3 4.0 concatenate.269
  285.8 3.6 fusion.20
  322.5 9.0 %fusion.29 = bf16[4,1024,64]{1,2,0:T(8,128)(2,1)} fusion(bf16[4,1024,64]{1,2,0:T(8,128)(2,1)S(1)} %bitcast.186, f32[4,1024,1024]{1,2,0:T(8,128)} %copy-done, f32[4,1024]{1,0:T(4,128)S(1)} %log_add_fusion, pred[1024,1024]{0,1:T(8,128)(4,1)S(1)} %or_and_fusion), kind=kOutput, calls=%fused_computation.102 | convolution fusion | flops 553910272 | bytes 18890752 | tf_op jit(solution)/shard_map/hqk,hqd->hkd/dot_general | solution.py:427
  331.5 12.1 %multiply_reduce_fusion = (f32[4,1024]{1,0:T(4,128)S(1)}, f32[4,1024,1024]{1,2,0:T(8,128)}) fusion(f32[4,1024,1024]{1,2,0:T(8,128)} %copy-done, f32[4,1024]{1,0:T(4,128)S(1)} %log_add_fusion, pred[1024,1024]{0,1:T(8,128)(4,1)S(1)} %or_and_fusion, bf16[4,1024,64]{1,2,0:T(8,128)(2,1)S(1)} %bitcast.187, bf16[4,1024,64]{1,2,0:T(8,128)(2,1)S(1)} %bitcast.189), kind=kOutput, calls=%fused_computation.1 | convolution fusion | flops 557838336 | bytes 35684352 | tf_op jit(solution)/shard_map/hqd,hkd->hqk/dot_general | solution.py:417
  343.6 12.2 %multiply_convert_fusion = bf16[4,1024,1024]{1,2,0:T(8,128)(2,1)S(1)} fusion(f32[4,1024,1024]{1,2,0:T(8,128)} %get-tuple-element.177, f32[4,1024,1024]{1,2,0:T(8,128)} %copy-done, f32[4,1024]{1,0:T(4,128)S(1)} %get-tuple-element.176, f32[4,1024]{1,0:T(4,128)S(1)} %log_add_fusion, pred[1024,1024]{0,1:T(8,128)(4,1)S(1)} %or_and_fusion), kind=kLoop, calls=%fused_computation | loop fusion | flops 25165824 | bytes 43024384 | tf_op jit(solution)/shard_map/convert_element_type | solution.py:419
  372.2 6.6 %collective-permute-done.31 = bf16[256,1024]{1,0:T(8,128)(2,1)S(1)} collective-permute-done((bf16[256,1024]{1,0:T(8,128)(2,1)S(1)}, bf16[256,1024]{1,0:T(8,128)(2,1)S(1)}, u32[]{:S(2)}, u32[]{:S(2)}) %collective-permute-start.31) | collective-permute-done | bytes 524320 | tf_op jit(solution)/shard_map/ppermute | solution.py:61
  380.2 10.7 %collective-permute-done.33 = bf16[256,1024]{1,0:T(8,128)(2,1)S(1)} collective-permute-done((bf16[256,1024]{1,0:T(8,128)(2,1)S(1)}, bf16[256,1024]{1,0:T(8,128)(2,1)S(1)}, u32[]{:S(2)}, u32[]{:S(2)}) %collective-permute-start.33) | collective-permute-done | bytes 524320 | tf_op jit(solution)/shard_map/ppermute | solution.py:61
  391.0 22.5 %collective-permute-done.32 = bf16[256,1024]{1,0:T(8,128)(2,1)S(1)} collective-permute-done((bf16[256,1024]{1,0:T(8,128)(2,1)S(1)}, bf16[256,1024]{1,0:T(8,128)(2,1)S(1)}, u32[]{:S(2)}, u32[]{:S(2)}) %collective-permute-start.32) | collective-permute-done | bytes 524320 | tf_op jit(solution)/shard_map/ppermute | solution.py:61
  426.6 3.3 convolution_convert_fusion.3
  434.5 3.1 collective-permute-done.36
  460.4 3.2 add_convert_fusion.24
  466.1 18.5 %collective-permute-done.53 = bf16[2,256,1024]{2,1,0:T(8,128)(2,1)S(1)} collective-permute-done((bf16[2,256,1024]{2,1,0:T(8,128)(2,1)S(1)}, bf16[2,256,1024]{2,1,0:T(8,128)(2,1)S(1)}, u32[]{:S(2)}, u32[]{:S(2)}) %collective-permute-start.53) | collective-permute-done | bytes 1048608 | tf_op jit(solution)/shard_map/ppermute | solution.py:61
  489.1 6.5 %collective-permute-done.43 = bf16[2,64,5120]{2,1,0:T(8,128)(2,1)S(1)} collective-permute-done((bf16[2,64,5120]{2,1,0:T(8,128)(2,1)S(1)}, bf16[2,64,5120]{2,1,0:T(8,128)(2,1)S(1)}, u32[]{:S(2)}, u32[]{:S(2)}) %collective-permute-start.43) | collective-permute-done | bytes 1310752 | tf_op jit(solution)/shard_map/ppermute | solution.py:61
  496.1 16.7 %collective-permute-done.45 = bf16[2,64,5120]{2,1,0:T(8,128)(2,1)S(1)} collective-permute-done((bf16[2,64,5120]{2,1,0:T(8,128)(2,1)S(1)}, bf16[2,64,5120]{2,1,0:T(8,128)(2,1)S(1)}, u32[]{:S(2)}, u32[]{:S(2)}) %collective-permute-start.45) | collective-permute-done | bytes 1310752 | tf_op jit(solution)/shard_map/ppermute | solution.py:61
  514.6 8.4 %collective-permute-done.44 = bf16[1,64,5120]{2,1,0:T(8,128)(2,1)S(1)} collective-permute-done((bf16[1,64,5120]{2,1,0:T(8,128)(2,1)S(1)}, bf16[1,64,5120]{2,1,0:T(8,128)(2,1)S(1)}, u32[]{:S(2)}, u32[]{:S(2)}) %collective-permute-start.44) | collective-permute-done | bytes 655392 | tf_op jit(solution)/shard_map/ppermute | solution.py:61
  523.3 15.9 %collective-permute-done.46 = bf16[1,64,5120]{2,1,0:T(8,128)(2,1)S(1)} collective-permute-done((bf16[1,64,5120]{2,1,0:T(8,128)(2,1)S(1)}, bf16[1,64,5120]{2,1,0:T(8,128)(2,1)S(1)}, u32[]{:S(2)}, u32[]{:S(2)}) %collective-permute-start.46) | collective-permute-done | bytes 655392 | tf_op jit(solution)/shard_map/ppermute | solution.py:61
  546.9 4.5 collective-permute-done.52
  556.9 4.8 collective-permute-start.57
  561.6 9.1 %collective-permute-done.48 = bf16[32,5120]{1,0:T(8,128)(2,1)S(1)} collective-permute-done((bf16[32,5120]{1,0:T(8,128)(2,1)S(1)}, bf16[32,5120]{1,0:T(8,128)(2,1)S(1)}, u32[]{:S(2)}, u32[]{:S(2)}) %collective-permute-start.48) | collective-permute-done | bytes 327712 | tf_op jit(solution)/shard_map/ppermute | solution.py:61
  572.6 18.0 %collective-permute-done.56 = bf16[128,1024]{1,0:T(8,128)(2,1)S(1)} collective-permute-done((bf16[128,1024]{1,0:T(8,128)(2,1)S(1)}, bf16[128,1024]{1,0:T(8,128)(2,1)S(1)}, u32[]{:S(2)}, u32[]{:S(2)}) %collective-permute-start.56) | collective-permute-done | bytes 262176 | tf_op jit(solution)/shard_map/ppermute | solution.py:61
  (470 shorter events, 213.3 us)
Async XLA Ops:
  2.5 45.4 %collective-permute-start.4 = (bf16[32,5120]{1,0:T(8,128)(2,1)S(1)}, bf16[32,5120]{1,0:T(8,128)(2,1)S(1)}, u32[]{:S(2)}, u32[]{:S(2)}) collective-permute-start(bf16[32,5120]{1,0:T(8,128)(2,1)S(1)} %constant_dynamic-update-slice_fusion), channel_id=1, source_target_pairs={{0,3},{1,2},{2,1},{3,0},{4,7},{5,6},{6,5},{7,4},{8,11},{9,10},{10,... | collective-permute-start | bytes 983048 | tf_op jit(solution)/shard_map/ppermute | solution.py:61
  7.6 40.2 %collective-permute-start.2 = (bf16[32,5120]{1,0:T(8,128)(2,1)S(1)}, bf16[32,5120]{1,0:T(8,128)(2,1)S(1)}, u32[]{:S(2)}, u32[]{:S(2)}) collective-permute-start(bf16[32,5120]{1,0:T(8,128)(2,1)S(1)} %constant_dynamic-update-slice_fusion), channel_id=1, source_target_pairs={{0,2},{1,3},{2,0},{3,1},{4,6},{5,7},{6,4},{7,5},{8,10},{9,11},{10,... | collective-permute-start | bytes 983048 | tf_op jit(solution)/shard_map/ppermute | solution.py:61
  15.5 24.3 %collective-permute-start.7 = (bf16[32,896]{1,0:T(8,128)(2,1)S(1)}, bf16[32,896]{1,0:T(8,128)(2,1)S(1)}, u32[]{:S(2)}, u32[]{:S(2)}) collective-permute-start(bf16[32,896]{1,0:T(8,128)(2,1)S(1)} %get-tuple-element.159), channel_id=1, source_target_pairs={{0,2},{1,3},{2,0},{3,1},{4,6},{5,7},{6,4},{7,5},{8,10},{9,11},{10,... | collective-permute-start | bytes 172040 | tf_op jit(solution)/shard_map/ppermute | solution.py:61
  18.5 21.4 %collective-permute-start.8 = (bf16[32,896]{1,0:T(8,128)(2,1)S(1)}, bf16[32,896]{1,0:T(8,128)(2,1)S(1)}, u32[]{:S(2)}, u32[]{:S(2)}) collective-permute-start(bf16[32,896]{1,0:T(8,128)(2,1)S(1)} %get-tuple-element.160), channel_id=1, source_target_pairs={{0,1},{1,0},{2,3},{3,2},{4,5},{5,4},{6,7},{7,6},{8,9},{9,8},{10,11... | collective-permute-start | bytes 172040 | tf_op jit(solution)/shard_map/ppermute | solution.py:61
  18.5 21.4 %collective-permute-start.6 = (bf16[32,896]{1,0:T(8,128)(2,1)S(1)}, bf16[32,896]{1,0:T(8,128)(2,1)S(1)}, u32[]{:S(2)}, u32[]{:S(2)}) collective-permute-start(bf16[32,896]{1,0:T(8,128)(2,1)S(1)} %get-tuple-element.161), channel_id=1, source_target_pairs={{0,3},{1,2},{2,1},{3,0},{4,7},{5,6},{6,5},{7,4},{8,11},{9,10},{10,... | collective-permute-start | bytes 172040 | tf_op jit(solution)/shard_map/ppermute | solution.py:61
  48.0 20.7 %collective-permute-start.1 = (bf16[256,1024]{1,0:T(8,128)(2,1)S(1)}, bf16[256,1024]{1,0:T(8,128)(2,1)S(1)}, u32[]{:S(2)}, u32[]{:S(2)}) collective-permute-start(bf16[256,1024]{1,0:T(8,128)(2,1)S(1)} %copy-done.3), channel_id=1, source_target_pairs={{0,1},{1,0},{2,3},{3,2},{4,5},{5,4},{6,7},{7,6},{8,9},{9,8},{10,11... | collective-permute-start | bytes 1572872 | tf_op jit(solution)/shard_map/ppermute | solution.py:61
  49.9 38.2 %collective-permute-start.3 = (bf16[256,1024]{1,0:T(8,128)(2,1)S(1)}, bf16[256,1024]{1,0:T(8,128)(2,1)S(1)}, u32[]{:S(2)}, u32[]{:S(2)}) collective-permute-start(bf16[256,1024]{1,0:T(8,128)(2,1)S(1)} %copy-done.3), channel_id=1, source_target_pairs={{0,2},{1,3},{2,0},{3,1},{4,6},{5,7},{6,4},{7,5},{8,10},{9,11},{10,... | collective-permute-start | bytes 1572872 | tf_op jit(solution)/shard_map/ppermute | solution.py:61
  51.0 37.1 %collective-permute-start.5 = (bf16[256,1024]{1,0:T(8,128)(2,1)S(1)}, bf16[256,1024]{1,0:T(8,128)(2,1)S(1)}, u32[]{:S(2)}, u32[]{:S(2)}) collective-permute-start(bf16[256,1024]{1,0:T(8,128)(2,1)S(1)} %copy-done.3), channel_id=1, source_target_pairs={{0,3},{1,2},{2,1},{3,0},{4,7},{5,6},{6,5},{7,4},{8,11},{9,10},{10,... | collective-permute-start | bytes 1572872 | tf_op jit(solution)/shard_map/ppermute | solution.py:61
  54.3 55.3 %collective-permute-start.15 = (bf16[64,5120]{1,0:T(8,128)(2,1)S(1)}, bf16[64,5120]{1,0:T(8,128)(2,1)S(1)}, u32[]{:S(2)}, u32[]{:S(2)}) collective-permute-start(bf16[64,5120]{1,0:T(8,128)(2,1)S(1)} %pad_maximum_fusion.11), channel_id=1, source_target_pairs={{0,8},{4,12},{8,0},{12,4},{16,24},{20,28},{24,16},{28,20},{1,9},{5... | collective-permute-start | bytes 1966088 | tf_op jit(solution)/shard_map/ppermute | solution.py:61
  57.7 49.7 %collective-permute-start.16 = (bf16[64,5120]{1,0:T(8,128)(2,1)S(1)}, bf16[64,5120]{1,0:T(8,128)(2,1)S(1)}, u32[]{:S(2)}, u32[]{:S(2)}) collective-permute-start(bf16[64,5120]{1,0:T(8,128)(2,1)S(1)} %pad_maximum_fusion.12), channel_id=1, source_target_pairs={{0,16},{4,20},{8,24},{12,28},{16,0},{20,4},{24,8},{28,12},{1,17},{... | collective-permute-start | bytes 1966088 | tf_op jit(solution)/shard_map/ppermute | solution.py:61
  68.7 85.1 %collective-permute-start.11 = (bf16[512,896]{1,0:T(8,128)(2,1)S(1)}, bf16[512,896]{1,0:T(8,128)(2,1)S(1)}, u32[]{:S(2)}, u32[]{:S(2)}) collective-permute-start(bf16[512,896]{1,0:T(8,128)(2,1)S(1)} %constant_dynamic-update-slice_fusion.7), channel_id=1, source_target_pairs={{0,4},{4,0},{8,12},{12,8},{16,20},{20,16},{24,28},{28,24},{1,5},{5... | collective-permute-start | bytes 2752520 | tf_op jit(solution)/shard_map/ppermute | solution.py:61
  88.1 24.1 %collective-permute-start.22 = (bf16[128,1024]{1,0:T(8,128)(2,1)S(1)}, bf16[128,1024]{1,0:T(8,128)(2,1)S(1)}, u32[]{:S(2)}, u32[]{:S(2)}) collective-permute-start(bf16[128,1024]{1,0:T(8,128)(2,1)S(1)} %copy-done.29), channel_id=1, source_target_pairs={{0,1},{1,0},{2,3},{3,2},{4,5},{5,4},{6,7},{7,6},{8,9},{9,8},{10,11... | collective-permute-start | bytes 786440 | tf_op jit(solution)/shard_map/ppermute | solution.py:61
  88.2 25.1 %collective-permute-start.21 = (bf16[128,1024]{1,0:T(8,128)(2,1)S(1)}, bf16[128,1024]{1,0:T(8,128)(2,1)S(1)}, u32[]{:S(2)}, u32[]{:S(2)}) collective-permute-start(bf16[128,1024]{1,0:T(8,128)(2,1)S(1)} %copy-done.29), channel_id=1, source_target_pairs={{0,2},{1,3},{2,0},{3,1},{4,6},{5,7},{6,4},{7,5},{8,10},{9,11},{10,... | collective-permute-start | bytes 786440 | tf_op jit(solution)/shard_map/ppermute | solution.py:61
  109.6 54.0 %collective-permute-start.17 = (bf16[128,5120]{1,0:T(8,128)(2,1)}, bf16[128,5120]{1,0:T(8,128)(2,1)}, u32[]{:S(2)}, u32[]{:S(2)}) collective-permute-start(bf16[128,5120]{1,0:T(8,128)(2,1)} %pad_maximum_fusion.2), channel_id=1, source_target_pairs={{0,8},{4,12},{8,0},{12,4},{16,24},{20,28},{24,16},{28,20},{1,9},{5... | collective-permute-start | bytes 3932168 | tf_op jit(solution)/shard_map/ppermute | solution.py:61
  112.3 54.5 %collective-permute-start.18 = (bf16[128,5120]{1,0:T(8,128)(2,1)}, bf16[128,5120]{1,0:T(8,128)(2,1)}, u32[]{:S(2)}, u32[]{:S(2)}) collective-permute-start(bf16[128,5120]{1,0:T(8,128)(2,1)} %pad_maximum_fusion.3), channel_id=1, source_target_pairs={{0,16},{4,20},{8,24},{12,28},{16,0},{20,4},{24,8},{28,12},{1,17},{... | collective-permute-start | bytes 3932168 | tf_op jit(solution)/shard_map/ppermute | solution.py:61
  117.6 33.6 %collective-permute-start.23 = (bf16[256,1024]{1,0:T(8,128)(2,1)S(1)}, bf16[256,1024]{1,0:T(8,128)(2,1)S(1)}, u32[]{:S(2)}, u32[]{:S(2)}) collective-permute-start(bf16[256,1024]{1,0:T(8,128)(2,1)S(1)} %pad_maximum_fusion.15), channel_id=1, source_target_pairs={{0,8},{4,12},{8,0},{12,4},{16,24},{20,28},{24,16},{28,20},{1,9},{5... | collective-permute-start | bytes 1572872 | tf_op jit(solution)/shard_map/ppermute | solution.py:61
  120.9 29.1 %collective-permute-start.24 = (bf16[256,1024]{1,0:T(8,128)(2,1)S(1)}, bf16[256,1024]{1,0:T(8,128)(2,1)S(1)}, u32[]{:S(2)}, u32[]{:S(2)}) collective-permute-start(bf16[256,1024]{1,0:T(8,128)(2,1)S(1)} %pad_maximum_fusion.16), channel_id=1, source_target_pairs={{0,16},{4,20},{8,24},{12,28},{16,0},{20,4},{24,8},{28,12},{1,17},{... | collective-permute-start | bytes 1572872 | tf_op jit(solution)/shard_map/ppermute | solution.py:61
  151.1 23.5 %collective-permute-start.25 = (bf16[512,1024]{1,0:T(8,128)(2,1)}, bf16[512,1024]{1,0:T(8,128)(2,1)}, u32[]{:S(2)}, u32[]{:S(2)}) collective-permute-start(bf16[512,1024]{1,0:T(8,128)(2,1)} %pad_maximum_fusion.6), channel_id=1, source_target_pairs={{0,8},{4,12},{8,0},{12,4},{16,24},{20,28},{24,16},{28,20},{1,9},{5... | collective-permute-start | bytes 3145736 | tf_op jit(solution)/shard_map/ppermute | solution.py:61
  152.2 24.3 %collective-permute-start.26 = (bf16[512,1024]{1,0:T(8,128)(2,1)}, bf16[512,1024]{1,0:T(8,128)(2,1)}, u32[]{:S(2)}, u32[]{:S(2)}) collective-permute-start(bf16[512,1024]{1,0:T(8,128)(2,1)} %pad_maximum_fusion.7), channel_id=1, source_target_pairs={{0,16},{4,20},{8,24},{12,28},{16,0},{20,4},{24,8},{28,12},{1,17},{... | collective-permute-start | bytes 3145736 | tf_op jit(solution)/shard_map/ppermute | solution.py:61
  174.6 48.3 %collective-permute-start.19 = (bf16[512,5120]{1,0:T(8,128)(2,1)}, bf16[512,5120]{1,0:T(8,128)(2,1)}, u32[]{:S(2)}, u32[]{:S(2)}) collective-permute-start(bf16[512,5120]{1,0:T(8,128)(2,1)} %slice_dynamic-update-slice_fusion), channel_id=1, source_target_pairs={{0,4},{4,0},{8,12},{12,8},{16,20},{20,16},{24,28},{28,24},{1,5},{5... | collective-permute-start | bytes 15728648 | tf_op jit(solution)/shard_map/ppermute | solution.py:61
  183.0 35.0 %collective-permute-start.27 = (bf16[2048,1024]{1,0:T(8,128)(2,1)}, bf16[2048,1024]{1,0:T(8,128)(2,1)}, u32[]{:S(2)}, u32[]{:S(2)}) collective-permute-start(bf16[2048,1024]{1,0:T(8,128)(2,1)} %slice_dynamic-update-slice_fusion.4), channel_id=1, source_target_pairs={{0,4},{4,0},{8,12},{12,8},{16,20},{20,16},{24,28},{28,24},{1,5},{5... | collective-permute-start | bytes 12582920 | tf_op jit(solution)/shard_map/ppermute | solution.py:61
  197.3 13.0 %collective-permute-start.13 = (bf16[256,256]{1,0:T(8,128)(2,1)S(1)}, bf16[256,256]{1,0:T(8,128)(2,1)S(1)}, u32[]{:S(2)}, u32[]{:S(2)}) collective-permute-start(bf16[256,256]{1,0:T(8,128)(2,1)S(1)} %copy.94), channel_id=1, source_target_pairs={{0,2},{1,3},{2,0},{3,1},{4,6},{5,7},{6,4},{7,5},{8,10},{9,11},{10,... | collective-permute-start | bytes 393224 | tf_op jit(solution)/shard_map/ppermute | solution.py:61
  285.8 23.4 %collective-permute-start.58 = (f32[1,128]{1,0:T(1,128)}, f32[1,128]{1,0:T(1,128)}, u32[]{:S(2)}, u32[]{:S(2)}) collective-permute-start(f32[1,128]{1,0:T(1,128)} %pad_bitcast_fusion.1), channel_id=1, source_target_pairs={{0,4},{4,0},{8,12},{12,8},{16,20},{20,16},{24,28},{28,24},{1,5},{5... | collective-permute-start | bytes 1544 | tf_op jit(solution)/shard_map/ppermute | solution.py:61
  304.7 14.2 %collective-permute-start.30 = (bf16[256,256]{1,0:T(8,128)(2,1)}, bf16[256,256]{1,0:T(8,128)(2,1)S(1)}, u32[]{:S(2)}, u32[]{:S(2)}) collective-permute-start(bf16[256,256]{1,0:T(8,128)(2,1)} %get-tuple-element.118), channel_id=1, source_target_pairs={{0,3},{1,2},{2,1},{3,0},{4,7},{5,6},{6,5},{7,4},{8,11},{9,10},{10,... | collective-permute-start | bytes 393224 | tf_op jit(solution)/shard_map/ppermute | solution.py:61
  306.8 14.4 %collective-permute-start.29 = (bf16[256,256]{1,0:T(8,128)(2,1)}, bf16[256,256]{1,0:T(8,128)(2,1)}, u32[]{:S(2)}, u32[]{:S(2)}) collective-permute-start(bf16[256,256]{1,0:T(8,128)(2,1)} %get-tuple-element.119), channel_id=1, source_target_pairs={{0,2},{1,3},{2,0},{3,1},{4,6},{5,7},{6,4},{7,5},{8,10},{9,11},{10,... | collective-permute-start | bytes 393224 | tf_op jit(solution)/shard_map/ppermute | solution.py:61
  308.6 12.6 %collective-permute-start.28 = (bf16[256,256]{1,0:T(8,128)(2,1)S(1)}, bf16[256,256]{1,0:T(8,128)(2,1)}, u32[]{:S(2)}, u32[]{:S(2)}) collective-permute-start(bf16[256,256]{1,0:T(8,128)(2,1)S(1)} %get-tuple-element.120), channel_id=1, source_target_pairs={{0,1},{1,0},{2,3},{3,2},{4,5},{5,4},{6,7},{7,6},{8,9},{9,8},{10,11... | collective-permute-start | bytes 393224 | tf_op jit(solution)/shard_map/ppermute | solution.py:61
  317.2 139.0 %collective-permute-start.50 = (bf16[2048,1024]{1,0:T(8,128)(2,1)}, bf16[2048,1024]{1,0:T(8,128)(2,1)}, u32[]{:S(2)}, u32[]{:S(2)}) collective-permute-start(bf16[2048,1024]{1,0:T(8,128)(2,1)} %convolution_convert_fusion.2), channel_id=1, source_target_pairs={{0,4},{4,0},{8,12},{12,8},{16,20},{20,16},{24,28},{28,24},{1,5},{5... | collective-permute-start | bytes 12582920 | tf_op jit(solution)/shard_map/ppermute | solution.py:61
  317.2 143.2 %collective-permute-start.42 = (bf16[512,4096]{1,0:T(8,128)(2,1)}, bf16[512,4096]{1,0:T(8,128)(2,1)}, u32[]{:S(2)}, u32[]{:S(2)}) collective-permute-start(bf16[512,4096]{1,0:T(8,128)(2,1)} %convolution_convert_fusion), channel_id=1, source_target_pairs={{0,4},{4,0},{8,12},{12,8},{16,20},{20,16},{24,28},{28,24},{1,5},{5... | collective-permute-start | bytes 12582920 | tf_op jit(solution)/shard_map/ppermute | solution.py:61
  364.7 14.2 %collective-permute-start.31 = (bf16[256,1024]{1,0:T(8,128)(2,1)S(1)}, bf16[256,1024]{1,0:T(8,128)(2,1)S(1)}, u32[]{:S(2)}, u32[]{:S(2)}) collective-permute-start(bf16[256,1024]{1,0:T(8,128)(2,1)S(1)} %get-tuple-element.99), channel_id=1, source_target_pairs={{0,1},{1,0},{2,3},{3,2},{4,5},{5,4},{6,7},{7,6},{8,9},{9,8},{10,11... | collective-permute-start | bytes 1572872 | tf_op jit(solution)/shard_map/ppermute | solution.py:61
  364.7 26.2 %collective-permute-start.33 = (bf16[256,1024]{1,0:T(8,128)(2,1)S(1)}, bf16[256,1024]{1,0:T(8,128)(2,1)S(1)}, u32[]{:S(2)}, u32[]{:S(2)}) collective-permute-start(bf16[256,1024]{1,0:T(8,128)(2,1)S(1)} %get-tuple-element.100), channel_id=1, source_target_pairs={{0,3},{1,2},{2,1},{3,0},{4,7},{5,6},{6,5},{7,4},{8,11},{9,10},{10,... | collective-permute-start | bytes 1572872 | tf_op jit(solution)/shard_map/ppermute | solution.py:61
  366.9 46.6 %collective-permute-start.32 = (bf16[256,1024]{1,0:T(8,128)(2,1)S(1)}, bf16[256,1024]{1,0:T(8,128)(2,1)S(1)}, u32[]{:S(2)}, u32[]{:S(2)}) collective-permute-start(bf16[256,1024]{1,0:T(8,128)(2,1)S(1)} %get-tuple-element.101), channel_id=1, source_target_pairs={{0,2},{1,3},{2,0},{3,1},{4,6},{5,7},{6,4},{7,5},{8,10},{9,11},{10,... | collective-permute-start | bytes 1572872 | tf_op jit(solution)/shard_map/ppermute | solution.py:61
  378.9 51.1 %collective-permute-start.60 = (f32[1,128]{1,0:T(1,128)S(1)}, f32[1,128]{1,0:T(1,128)S(1)}, u32[]{:S(2)}, u32[]{:S(2)}) collective-permute-start(f32[1,128]{1,0:T(1,128)S(1)} %copy-done.65), channel_id=1, source_target_pairs={{0,16},{4,20},{8,24},{12,28},{16,0},{20,4},{24,8},{28,12},{1,17},{... | collective-permute-start | bytes 1544 | tf_op jit(solution)/shard_map/ppermute | solution.py:61
  391.0 32.2 %collective-permute-start.34 = (bf16[512,768]{1,0:T(8,128)(2,1)}, bf16[512,768]{1,0:T(8,128)(2,1)}, u32[]{:S(2)}, u32[]{:S(2)}) collective-permute-start(bf16[512,768]{1,0:T(8,128)(2,1)} %convolution_convert_fusion.8), channel_id=1, source_target_pairs={{0,4},{4,0},{8,12},{12,8},{16,20},{20,16},{24,28},{28,24},{1,5},{5... | collective-permute-start | bytes 2359304 | tf_op jit(solution)/shard_map/ppermute | solution.py:61
  425.0 12.6 %collective-permute-start.36 = (bf16[2,128,896]{2,1,0:T(8,128)(2,1)S(1)}, bf16[2,128,896]{2,1,0:T(8,128)(2,1)S(1)}, u32[]{:S(2)}, u32[]{:S(2)}) collective-permute-start(bf16[2,128,896]{2,1,0:T(8,128)(2,1)S(1)} %pad_maximum_fusion.20), channel_id=1, source_target_pairs={{0,16},{4,20},{8,24},{12,28},{16,0},{20,4},{24,8},{28,12},{1,17},{... | collective-permute-start | bytes 1376264 | tf_op jit(solution)/shard_map/ppermute | solution.py:61
  430.4 17.0 %collective-permute-start.41 = (bf16[512,1024]{1,0:T(8,128)(2,1)S(1)}, bf16[512,1024]{1,0:T(8,128)(2,1)S(1)}, u32[]{:S(2)}, u32[]{:S(2)}) collective-permute-start(bf16[512,1024]{1,0:T(8,128)(2,1)S(1)} %convolution_convert_fusion.6), channel_id=1, source_target_pairs={{0,4},{4,0},{8,12},{12,8},{16,20},{20,16},{24,28},{28,24},{1,5},{5... | collective-permute-start | bytes 3145736 | tf_op jit(solution)/shard_map/ppermute | solution.py:61
  458.6 26.1 %collective-permute-start.53 = (bf16[2,256,1024]{2,1,0:T(8,128)(2,1)S(1)}, bf16[2,256,1024]{2,1,0:T(8,128)(2,1)S(1)}, u32[]{:S(2)}, u32[]{:S(2)}) collective-permute-start(bf16[2,256,1024]{2,1,0:T(8,128)(2,1)S(1)} %pad_maximum_fusion.10), channel_id=1, source_target_pairs={{0,8},{4,12},{8,0},{12,4},{16,24},{20,28},{24,16},{28,20},{1,9},{5... | collective-permute-start | bytes 3145736 | tf_op jit(solution)/shard_map/ppermute | solution.py:61
  463.9 31.7 %collective-permute-start.43 = (bf16[2,64,5120]{2,1,0:T(8,128)(2,1)S(1)}, bf16[2,64,5120]{2,1,0:T(8,128)(2,1)S(1)}, u32[]{:S(2)}, u32[]{:S(2)}) collective-permute-start(bf16[2,64,5120]{2,1,0:T(8,128)(2,1)S(1)} %pad_maximum_fusion.4), channel_id=1, source_target_pairs={{0,16},{4,20},{8,24},{12,28},{16,0},{20,4},{24,8},{28,12},{1,17},{... | collective-permute-start | bytes 3932168 | tf_op jit(solution)/shard_map/ppermute | solution.py:61
  465.7 47.0 %collective-permute-start.45 = (bf16[2,64,5120]{2,1,0:T(8,128)(2,1)S(1)}, bf16[2,64,5120]{2,1,0:T(8,128)(2,1)S(1)}, u32[]{:S(2)}, u32[]{:S(2)}) collective-permute-start(bf16[2,64,5120]{2,1,0:T(8,128)(2,1)S(1)} %pad_maximum_fusion.5), channel_id=1, source_target_pairs={{0,8},{4,12},{8,0},{12,4},{16,24},{20,28},{24,16},{28,20},{1,9},{5... | collective-permute-start | bytes 3932168 | tf_op jit(solution)/shard_map/ppermute | solution.py:61
  486.8 52.6 %collective-permute-start.54 = (bf16[1,256,1024]{2,1,0:T(8,128)(2,1)S(1)}, bf16[1,256,1024]{2,1,0:T(8,128)(2,1)S(1)}, u32[]{:S(2)}, u32[]{:S(2)}) collective-permute-start(bf16[1,256,1024]{2,1,0:T(8,128)(2,1)S(1)} %get-tuple-element.75), channel_id=1, source_target_pairs={{0,16},{4,20},{8,24},{12,28},{16,0},{20,4},{24,8},{28,12},{1,17},{... | collective-permute-start | bytes 1572872 | tf_op jit(solution)/shard_map/ppermute | solution.py:61
  488.6 50.9 %collective-permute-start.51 = (bf16[2,256,1024]{2,1,0:T(8,128)(2,1)S(1)}, bf16[2,256,1024]{2,1,0:T(8,128)(2,1)S(1)}, u32[]{:S(2)}, u32[]{:S(2)}) collective-permute-start(bf16[2,256,1024]{2,1,0:T(8,128)(2,1)S(1)} %pad_maximum_fusion.9), channel_id=1, source_target_pairs={{0,16},{4,20},{8,24},{12,28},{16,0},{20,4},{24,8},{28,12},{1,17},{... | collective-permute-start | bytes 3145736 | tf_op jit(solution)/shard_map/ppermute | solution.py:61
  495.8 27.3 %collective-permute-start.44 = (bf16[1,64,5120]{2,1,0:T(8,128)(2,1)S(1)}, bf16[1,64,5120]{2,1,0:T(8,128)(2,1)S(1)}, u32[]{:S(2)}, u32[]{:S(2)}) collective-permute-start(bf16[1,64,5120]{2,1,0:T(8,128)(2,1)S(1)} %add_convert_fusion.5), channel_id=1, source_target_pairs={{0,8},{4,12},{8,0},{12,4},{16,24},{20,28},{24,16},{28,20},{1,9},{5... | collective-permute-start | bytes 1966088 | tf_op jit(solution)/shard_map/ppermute | solution.py:61
  512.9 26.3 %collective-permute-start.46 = (bf16[1,64,5120]{2,1,0:T(8,128)(2,1)S(1)}, bf16[1,64,5120]{2,1,0:T(8,128)(2,1)S(1)}, u32[]{:S(2)}, u32[]{:S(2)}) collective-permute-start(bf16[1,64,5120]{2,1,0:T(8,128)(2,1)S(1)} %add_convert_fusion.2), channel_id=1, source_target_pairs={{0,16},{4,20},{8,24},{12,28},{16,0},{20,4},{24,8},{28,12},{1,17},{... | collective-permute-start | bytes 1966088 | tf_op jit(solution)/shard_map/ppermute | solution.py:61
  542.4 14.4 %collective-permute-start.47 = (bf16[32,5120]{1,0:T(8,128)(2,1)S(1)}, bf16[32,5120]{1,0:T(8,128)(2,1)S(1)}, u32[]{:S(2)}, u32[]{:S(2)}) collective-permute-start(bf16[32,5120]{1,0:T(8,128)(2,1)S(1)} %get-tuple-element.109), channel_id=1, source_target_pairs={{0,1},{1,0},{2,3},{3,2},{4,5},{5,4},{6,7},{7,6},{8,9},{9,8},{10,11... | collective-permute-start | bytes 983048 | tf_op jit(solution)/shard_map/ppermute | solution.py:61
  543.1 27.7 %collective-permute-start.48 = (bf16[32,5120]{1,0:T(8,128)(2,1)S(1)}, bf16[32,5120]{1,0:T(8,128)(2,1)S(1)}, u32[]{:S(2)}, u32[]{:S(2)}) collective-permute-start(bf16[32,5120]{1,0:T(8,128)(2,1)S(1)} %get-tuple-element.110), channel_id=1, source_target_pairs={{0,2},{1,3},{2,0},{3,1},{4,6},{5,7},{6,4},{7,5},{8,10},{9,11},{10,... | collective-permute-start | bytes 983048 | tf_op jit(solution)/shard_map/ppermute | solution.py:61
  545.4 25.4 %collective-permute-start.49 = (bf16[32,5120]{1,0:T(8,128)(2,1)S(1)}, bf16[32,5120]{1,0:T(8,128)(2,1)S(1)}, u32[]{:S(2)}, u32[]{:S(2)}) collective-permute-start(bf16[32,5120]{1,0:T(8,128)(2,1)S(1)} %get-tuple-element.111), channel_id=1, source_target_pairs={{0,3},{1,2},{2,1},{3,0},{4,7},{5,6},{6,5},{7,4},{8,11},{9,10},{10,... | collective-permute-start | bytes 983048 | tf_op jit(solution)/shard_map/ppermute | solution.py:61
  553.7 18.8 %collective-permute-start.55 = (bf16[128,1024]{1,0:T(8,128)(2,1)S(1)}, bf16[128,1024]{1,0:T(8,128)(2,1)S(1)}, u32[]{:S(2)}, u32[]{:S(2)}) collective-permute-start(bf16[128,1024]{1,0:T(8,128)(2,1)S(1)} %get-tuple-element.112), channel_id=1, source_target_pairs={{0,1},{1,0},{2,3},{3,2},{4,5},{5,4},{6,7},{7,6},{8,9},{9,8},{10,11... | collective-permute-start | bytes 786440 | tf_op jit(solution)/shard_map/ppermute | solution.py:61
  553.9 36.6 %collective-permute-start.56 = (bf16[128,1024]{1,0:T(8,128)(2,1)S(1)}, bf16[128,1024]{1,0:T(8,128)(2,1)S(1)}, u32[]{:S(2)}, u32[]{:S(2)}) collective-permute-start(bf16[128,1024]{1,0:T(8,128)(2,1)S(1)} %get-tuple-element.113), channel_id=1, source_target_pairs={{0,2},{1,3},{2,0},{3,1},{4,6},{5,7},{6,4},{7,5},{8,10},{9,11},{10,... | collective-permute-start | bytes 786440 | tf_op jit(solution)/shard_map/ppermute | solution.py:61
  556.9 33.6 %collective-permute-start.57 = (bf16[128,1024]{1,0:T(8,128)(2,1)S(1)}, bf16[128,1024]{1,0:T(8,128)(2,1)S(1)}, u32[]{:S(2)}, u32[]{:S(2)}) collective-permute-start(bf16[128,1024]{1,0:T(8,128)(2,1)S(1)} %get-tuple-element.114), channel_id=1, source_target_pairs={{0,3},{1,2},{2,1},{3,0},{4,7},{5,6},{6,5},{7,4},{8,11},{9,10},{10,... | collective-permute-start | bytes 786440 | tf_op jit(solution)/shard_map/ppermute | solution.py:61
  (81 other events, 1230.3 us)
